TPU v7x, 32 devices: a whole 2x2x4 slice. The times are simulated.
32 devices in a mesh: batch: 2 (over x), seq: 16 (over z, y, core).
Axes of the slice: x: 2, y: 2, z: 4, core: 2. Of those that a mesh axis runs over, the one named last changes fastest.
Arguments:
- frames: bfloat16 [1024, 4, 1024], P('seq', 'batch'), may hold values from -6 to 6
- cotangent: bfloat16 [1024, 4, 1024], P('seq', 'batch'), may hold values from -6 to 6
- segment_lengths: int32 [4, 4], P('batch'), may hold values from 1 to 832, 1024 in all within a row
- position_offsets: int32 [4, 4], P('batch'), may hold values from 0 to 1023
- first_gain: bfloat16 [1024], P('seq'), may hold values from 0.5 to 1.5
- first_shift: bfloat16 [1024], P('seq'), may hold values from -3 to 3
- inward_weight: bfloat16 [1024, 3072], P('seq'), may hold values from -0.1875 to 0.1875
- query_bias: bfloat16 [1024], P('seq'), may hold values from -3 to 3
- value_bias: bfloat16 [1024], P('seq'), may hold values from -3 to 3
- outward_weight: bfloat16 [1024, 1024], P('seq'), may hold values from -1.5 to 1.5
- outward_bias: bfloat16 [1024], P('seq'), may hold values from -3 to 3
- second_gain: bfloat16 [1024], P('seq'), may hold values from 0.5 to 1.5
- second_shift: bfloat16 [1024], P('seq'), may hold values from -3 to 3
- expand_weight: bfloat16 [1024, 4096], P('seq'), may hold values from -0.1875 to 0.1875
- expand_bias: bfloat16 [4096], P('seq'), may hold values from -3 to 3
- shrink_weight: bfloat16 [4096, 1024], P('seq'), may hold values from -0.09375 to 0.09375
- shrink_bias: bfloat16 [1024], P('seq'), may hold values from -3 to 3
Outputs:
- layer_output: bfloat16 [1024, 4, 1024], P('seq', 'batch')
- frames_grad: float32 [1024, 4, 1024], P('seq', 'batch')
- first_gain_grad: float32 [1024], P('seq')
- first_shift_grad: float32 [1024], P('seq')
- inward_weight_grad: float32 [1024, 3072], P('seq')
- query_bias_grad: float32 [1024], P('seq')
- value_bias_grad: float32 [1024], P('seq')
- outward_weight_grad: float32 [1024, 1024], P('seq')
- outward_bias_grad: float32 [1024], P('seq')
- second_gain_grad: float32 [1024], P('seq')
- second_shift_grad: float32 [1024], P('seq')
- expand_weight_grad: float32 [1024, 4096], P('seq')
- expand_bias_grad: float32 [4096], P('seq')
- shrink_weight_grad: float32 [4096, 1024], P('seq')
- shrink_bias_grad: float32 [1024], P('seq')
Inputs may be any that keep to these rules, and one draw needn't show every extreme that they name: `segment_lengths`: in each row the 4 lengths sum to 1024, and the largest is exactly 832.
All inputs are finite; a program needn't handle non-finite values.
Results may differ from a plain program's by a relative error of at most 0.011.
Values may be sent and summed in bfloat16 or wider, within the bound.
No kernel may reach another device: no remote copies, remote signals or barrier semaphores. Data moves between devices by JAX's collectives and lax.ppermute only.
A program may use at most 320 MiB of HBM per device.

v0:
```python
import math

import jax
import jax.numpy as jnp
from jax import lax
from jax.sharding import PartitionSpec as P

HEADS = 16


norm_eps = 1e-05


def layer_norm(values, gain, shift):
    center = values - jnp.mean(values, axis=-1, keepdims=True)
    spread = jnp.mean(center * center, axis=-1, keepdims=True)
    return center * lax.rsqrt(spread + norm_eps) * gain + shift


def smooth_gate(values):
    return jax.nn.gelu(values, approximate=True)


def frame_layout(frame_index, lengths, offsets):
    ends = jnp.cumsum(lengths, axis=1)
    starts = ends - lengths
    place = frame_index[:, None, None]
    inside = (place >= starts[None]) & (place < ends[None])
    labels = jnp.arange(lengths.shape[1], dtype=jnp.int32)
    segment = jnp.sum(jnp.where(inside, labels, 0), axis=2)
    position = jnp.sum(jnp.where(inside, offsets[None] + place - starts[None], 0), axis=2)
    return (segment, position)


def sinusoid(position, width):
    index = jnp.arange(width // 2, dtype=jnp.float32)
    rates = jnp.exp(index * (-2.0 * math.log(10000.0) / width))
    angles = position.astype(jnp.float32)[..., None] * rates
    return jnp.stack([jnp.sin(angles), jnp.cos(angles)], axis=-1).reshape(position.shape + (width,))


def pair_mask(query_place, query_segment, key_place, key_segment):
    same = query_segment.T[:, :, None] == key_segment.T[:, None, :]
    causal = query_place[:, None] >= key_place[None, :]
    return (same & causal[None])[:, None]


def score_block(queries, keys, scale_factor):
    return (
        jnp.einsum("irhd,jrhd->rhij", queries, keys, preferred_element_type=jnp.float32)
        * scale_factor
    )


def key_side(
    queries,
    context_grad,
    log_total,
    delta,
    query_place,
    query_segment,
    keys,
    values,
    key_place,
    key_segment,
    scale_factor,
):
    allowed = pair_mask(query_place, query_segment, key_place, key_segment)
    empty = jnp.zeros(keys.shape, jnp.float32)

    def work(unused):
        scores = score_block(queries, keys, scale_factor)
        probs = jnp.where(allowed, jnp.exp(scores - log_total[..., None]), 0.0)
        prob_grad = jnp.einsum(
            "irhd,jrhd->rhij", context_grad, values, preferred_element_type=jnp.float32
        )
        score_grad = (probs * (prob_grad - delta[..., None])).astype(jnp.bfloat16)
        key_grad = (
            jnp.einsum("rhij,irhd->jrhd", score_grad, queries, preferred_element_type=jnp.float32)
            * scale_factor
        )
        value_grad = jnp.einsum(
            "rhij,irhd->jrhd",
            probs.astype(jnp.bfloat16),
            context_grad,
            preferred_element_type=jnp.float32,
        )
        return (key_grad, value_grad)

    def skip(unused):
        return (empty, empty)

    return lax.cond(jnp.any(allowed), work, skip, 0)


def on_device(
    frames,
    cotangent,
    segment_lengths,
    position_offsets,
    first_gain,
    first_shift,
    inward_weight,
    query_bias,
    value_bias,
    outward_weight,
    outward_bias,
    second_gain,
    second_shift,
    expand_weight,
    expand_bias,
    shrink_weight,
    shrink_bias,
):
    gathered = (
        lax.all_gather(first_gain, "seq", axis=0, tiled=True),
        lax.all_gather(first_shift, "seq", axis=0, tiled=True),
        lax.all_gather(inward_weight, "seq", axis=0, tiled=True),
        lax.all_gather(query_bias, "seq", axis=0, tiled=True),
        lax.all_gather(value_bias, "seq", axis=0, tiled=True),
        lax.all_gather(outward_weight, "seq", axis=0, tiled=True),
        lax.all_gather(outward_bias, "seq", axis=0, tiled=True),
        lax.all_gather(second_gain, "seq", axis=0, tiled=True),
        lax.all_gather(second_shift, "seq", axis=0, tiled=True),
        lax.all_gather(expand_weight, "seq", axis=0, tiled=True),
        lax.all_gather(expand_bias, "seq", axis=0, tiled=True),
        lax.all_gather(shrink_weight, "seq", axis=0, tiled=True),
        lax.all_gather(shrink_bias, "seq", axis=0, tiled=True),
    )
    (
        gain_one,
        shift_one,
        inward,
        query_b,
        value_b,
        outward,
        outward_b,
        gain_two,
        shift_two,
        expand,
        expand_b,
        shrink,
        shrink_b,
    ) = gathered
    gain_one = gain_one.astype(jnp.float32)
    shift_one = shift_one.astype(jnp.float32)
    query_b = query_b.astype(jnp.float32)
    value_b = value_b.astype(jnp.float32)
    outward_b = outward_b.astype(jnp.float32)
    gain_two = gain_two.astype(jnp.float32)
    shift_two = shift_two.astype(jnp.float32)
    expand_b = expand_b.astype(jnp.float32)
    shrink_b = shrink_b.astype(jnp.float32)
    local_len, rows, width = frames.shape
    head_dim = width // HEADS
    seq_count = lax.axis_size("seq")
    seq_index = lax.axis_index("seq")
    full_len = local_len * seq_count
    block = min(512, full_len)
    block_count = full_len // block
    scale_factor = 1.0 / math.sqrt(head_dim)
    tokens = local_len * rows
    all_place = jnp.arange(full_len, dtype=jnp.int32)
    all_segment, all_position = frame_layout(all_place, segment_lengths, position_offsets)
    first_frame = seq_index * local_len
    my_place = first_frame + jnp.arange(local_len, dtype=jnp.int32)
    my_segment = lax.dynamic_slice_in_dim(all_segment, first_frame, local_len, 0)
    my_position = lax.dynamic_slice_in_dim(all_position, first_frame, local_len, 0)
    inputs = (frames.astype(jnp.float32) + sinusoid(my_position, width)).reshape(tokens, width)
    normed_f, first_back = jax.vjp(layer_norm, inputs, gain_one, shift_one)
    normed = normed_f.astype(jnp.bfloat16)
    mixed = jnp.dot(normed, inward, preferred_element_type=jnp.float32)
    query_rows = (mixed[:, :width] + query_b).astype(jnp.bfloat16)
    key_rows = mixed[:, width : 2 * width].astype(jnp.bfloat16)
    value_rows = (mixed[:, 2 * width :] + value_b).astype(jnp.bfloat16)
    queries = query_rows.reshape(local_len, rows, HEADS, head_dim)
    all_keys, all_values = (
        lax.all_gather(key_rows.reshape(local_len, rows, width), "seq", axis=0, tiled=True),
        lax.all_gather(value_rows.reshape(local_len, rows, width), "seq", axis=0, tiled=True),
    )
    all_keys = all_keys.reshape(full_len, rows, HEADS, head_dim)
    all_values = all_values.reshape(full_len, rows, HEADS, head_dim)

    def key_block(start, size):
        keys = lax.dynamic_slice_in_dim(all_keys, start, size, 0)
        values = lax.dynamic_slice_in_dim(all_values, start, size, 0)
        place = start + jnp.arange(size, dtype=jnp.int32)
        segment = lax.dynamic_slice_in_dim(all_segment, start, size, 0)
        return (keys, values, place, segment)

    def stats_step(index, carry):
        keys, values, place, segment = key_block(jnp.asarray(index, jnp.int32) * block, block)
        allowed = pair_mask(my_place, my_segment, place, segment)

        def stats_update(state):
            top, total = state
            scores = jnp.where(allowed, score_block(queries, keys, scale_factor), -1e30)
            new_top = jnp.maximum(top, jnp.max(scores, axis=-1))
            weights = jnp.where(allowed, jnp.exp(scores - new_top[..., None]), 0.0)
            return (new_top, total * jnp.exp(top - new_top) + jnp.sum(weights, axis=-1))

        return lax.cond(jnp.any(allowed), stats_update, lambda state: state, carry)

    top_start = jnp.full((rows, HEADS, local_len), -1e30, jnp.float32)
    total_start = jnp.zeros((rows, HEADS, local_len), jnp.float32)
    top, total = lax.fori_loop(0, block_count, stats_step, (top_start, total_start))
    log_total = top + jnp.log(total)

    def context_step(index, carry):
        keys, values, place, segment = key_block(jnp.asarray(index, jnp.int32) * block, block)
        allowed = pair_mask(my_place, my_segment, place, segment)

        def context_update(accum):
            probs = jnp.where(
                allowed,
                jnp.exp(score_block(queries, keys, scale_factor) - log_total[..., None]),
                0.0,
            )
            return accum + jnp.einsum(
                "rhij,jrhd->rhid",
                probs.astype(jnp.bfloat16),
                values,
                preferred_element_type=jnp.float32,
            )

        return lax.cond(jnp.any(allowed), context_update, lambda accum: accum, carry)

    context_acc = lax.fori_loop(
        0, block_count, context_step, jnp.zeros((rows, HEADS, local_len, head_dim), jnp.float32)
    )
    context = jnp.transpose(context_acc, (2, 0, 1, 3)).reshape(tokens, width).astype(jnp.bfloat16)
    middle = inputs + jnp.dot(context, outward, preferred_element_type=jnp.float32) + outward_b
    second_f, second_back = jax.vjp(layer_norm, middle, gain_two, shift_two)
    second_normed = second_f.astype(jnp.bfloat16)
    before = jnp.dot(second_normed, expand, preferred_element_type=jnp.float32) + expand_b
    active_f, gate_back = jax.vjp(smooth_gate, before)
    active = active_f.astype(jnp.bfloat16)
    result = middle + jnp.dot(active, shrink, preferred_element_type=jnp.float32) + shrink_b
    layer_output = result.reshape(local_len, rows, width).astype(jnp.bfloat16)
    upstream = cotangent.reshape(tokens, width)
    shrink_grad = jnp.einsum("nf,nd->fd", active, upstream, preferred_element_type=jnp.float32)
    shrink_b_grad = jnp.sum(upstream.astype(jnp.float32), axis=0)
    active_grad = jnp.einsum("nd,fd->nf", upstream, shrink, preferred_element_type=jnp.float32)
    before_grad = gate_back(active_grad)[0].astype(jnp.bfloat16)
    expand_grad = jnp.einsum(
        "nd,nf->df", second_normed, before_grad, preferred_element_type=jnp.float32
    )
    expand_b_grad = jnp.sum(before_grad.astype(jnp.float32), axis=0)
    second_grad = jnp.einsum("nf,df->nd", before_grad, expand, preferred_element_type=jnp.float32)
    middle_part, gain_two_grad, shift_two_grad = second_back(second_grad)
    ffn_sums = (
        lax.psum_scatter(gain_two_grad, "seq", scatter_dimension=0, tiled=True),
        lax.psum_scatter(shift_two_grad, "seq", scatter_dimension=0, tiled=True),
        lax.psum_scatter(expand_grad, "seq", scatter_dimension=0, tiled=True),
        lax.psum_scatter(expand_b_grad, "seq", scatter_dimension=0, tiled=True),
        lax.psum_scatter(shrink_grad, "seq", scatter_dimension=0, tiled=True),
        lax.psum_scatter(shrink_b_grad, "seq", scatter_dimension=0, tiled=True),
    )
    middle_grad = upstream.astype(jnp.float32) + middle_part
    low_middle = middle_grad.astype(jnp.bfloat16)
    outward_grad = jnp.einsum("nd,ne->de", context, low_middle, preferred_element_type=jnp.float32)
    outward_b_grad = jnp.sum(low_middle.astype(jnp.float32), axis=0)
    context_grad = jnp.einsum(
        "ne,de->nd", low_middle, outward, preferred_element_type=jnp.float32
    ).astype(jnp.bfloat16)
    context_grad = context_grad.reshape(local_len, rows, HEADS, head_dim)

    def delta_step(index, carry):
        keys, values, place, segment = key_block(jnp.asarray(index, jnp.int32) * block, block)
        allowed = pair_mask(my_place, my_segment, place, segment)

        def delta_update(accum):
            probs = jnp.where(
                allowed,
                jnp.exp(score_block(queries, keys, scale_factor) - log_total[..., None]),
                0.0,
            )
            prob_grad = jnp.einsum(
                "irhd,jrhd->rhij", context_grad, values, preferred_element_type=jnp.float32
            )
            return accum + jnp.sum(probs * prob_grad, axis=-1)

        return lax.cond(jnp.any(allowed), delta_update, lambda accum: accum, carry)

    delta = lax.fori_loop(
        0, block_count, delta_step, jnp.zeros((rows, HEADS, local_len), jnp.float32)
    )

    def query_step(index, carry):
        keys, values, place, segment = key_block(jnp.asarray(index, jnp.int32) * block, block)
        allowed = pair_mask(my_place, my_segment, place, segment)

        def query_update(accum):
            probs = jnp.where(
                allowed,
                jnp.exp(score_block(queries, keys, scale_factor) - log_total[..., None]),
                0.0,
            )
            prob_grad = jnp.einsum(
                "irhd,jrhd->rhij", context_grad, values, preferred_element_type=jnp.float32
            )
            score_grad = (probs * (prob_grad - delta[..., None])).astype(jnp.bfloat16)
            return accum + jnp.einsum(
                "rhij,jrhd->irhd", score_grad, keys, preferred_element_type=jnp.float32
            )

        return lax.cond(jnp.any(allowed), query_update, lambda accum: accum, carry)

    query_acc = lax.fori_loop(
        0, block_count, query_step, jnp.zeros((local_len, rows, HEADS, head_dim), jnp.float32)
    )
    query_grad = (query_acc * scale_factor).reshape(tokens, width).astype(jnp.bfloat16)
    count = local_len * lax.axis_size("seq")
    piece = math.gcd(count, block)
    steps = count // piece

    def one(step):
        keys, values, place, segment = key_block(step * piece, piece)
        key_grad, value_grad = key_side(
            queries,
            context_grad,
            log_total,
            delta,
            my_place,
            my_segment,
            keys,
            values,
            place,
            segment,
            scale_factor,
        )
        return jnp.concatenate(
            [key_grad.reshape(piece, rows, width), value_grad.reshape(piece, rows, width)], axis=2
        )

    parts = lax.map(one, jnp.arange(steps, dtype=jnp.int32))
    summed = lax.psum_scatter(
        parts.reshape(count, rows, 2 * width), "seq", scatter_dimension=0, tiled=True
    )
    key_sum = summed[:, :, :width]
    value_sum = summed[:, :, width:]
    key_grad_rows = key_sum.reshape(tokens, width).astype(jnp.bfloat16)
    value_grad_rows = value_sum.reshape(tokens, width).astype(jnp.bfloat16)
    mixed_grad = jnp.concatenate([query_grad, key_grad_rows, value_grad_rows], axis=1)
    inward_grad = jnp.einsum("nd,ne->de", normed, mixed_grad, preferred_element_type=jnp.float32)
    query_b_grad = jnp.sum(query_grad.astype(jnp.float32), axis=0)
    value_b_grad = jnp.sum(value_grad_rows.astype(jnp.float32), axis=0)
    normed_grad = jnp.einsum("ne,de->nd", mixed_grad, inward, preferred_element_type=jnp.float32)
    input_part, gain_one_grad, shift_one_grad = first_back(normed_grad)
    frames_grad = (middle_grad + input_part).reshape(local_len, rows, width)
    attn_sums = (
        lax.psum_scatter(gain_one_grad, "seq", scatter_dimension=0, tiled=True),
        lax.psum_scatter(shift_one_grad, "seq", scatter_dimension=0, tiled=True),
        lax.psum_scatter(inward_grad, "seq", scatter_dimension=0, tiled=True),
        lax.psum_scatter(query_b_grad, "seq", scatter_dimension=0, tiled=True),
        lax.psum_scatter(value_b_grad, "seq", scatter_dimension=0, tiled=True),
        lax.psum_scatter(outward_grad, "seq", scatter_dimension=0, tiled=True),
        lax.psum_scatter(outward_b_grad, "seq", scatter_dimension=0, tiled=True),
    )
    g_one, s_one, g_inward, g_query, g_value, g_outward, g_outward_b = attn_sums
    g_two, s_two, g_expand, g_expand_b, g_shrink, g_shrink_b = ffn_sums
    totals = lax.psum(
        (
            g_one,
            s_one,
            g_inward,
            g_query,
            g_value,
            g_outward,
            g_outward_b,
            g_two,
            s_two,
            g_expand,
            g_expand_b,
            g_shrink,
            g_shrink_b,
        ),
        "batch",
    )
    (
        g_one,
        s_one,
        g_inward,
        g_query,
        g_value,
        g_outward,
        g_outward_b,
        g_two,
        s_two,
        g_expand,
        g_expand_b,
        g_shrink,
        g_shrink_b,
    ) = totals
    return (
        layer_output,
        frames_grad,
        g_one,
        s_one,
        g_inward,
        g_query,
        g_value,
        g_outward,
        g_outward_b,
        g_two,
        s_two,
        g_expand,
        g_expand_b,
        g_shrink,
        g_shrink_b,
    )


def solution(mesh):
    in_specs = (
        P("seq", "batch", None),
        P("seq", "batch", None),
        P("batch", None),
        P("batch", None),
        P("seq"),
        P("seq"),
        P("seq", None),
        P("seq"),
        P("seq"),
        P("seq", None),
        P("seq"),
        P("seq"),
        P("seq"),
        P("seq", None),
        P("seq"),
        P("seq", None),
        P("seq"),
    )
    out_specs = (
        P("seq", "batch", None),
        P("seq", "batch", None),
        P("seq"),
        P("seq"),
        P("seq", None),
        P("seq"),
        P("seq"),
        P("seq", None),
        P("seq"),
        P("seq"),
        P("seq"),
        P("seq", None),
        P("seq"),
        P("seq", None),
        P("seq"),
    )
    return jax.shard_map(
        on_device, mesh=mesh, in_specs=in_specs, out_specs=out_specs, check_vma=False
    )
```

profile of v0, /device:TPU:0, one launch (start us, length us, event | category | flops | bytes accessed | tf_op | source)
XLA Modules:
  0.0 1348.9 jit_solution(2382722913252642953)
XLA Ops:
  10.3 1.3 fusion.104
  18.9 63.9 %all-reduce.20 = (bf16[1024]{0:T(1024)(128)(2,1)S(1)}, bf16[1024]{0:T(1024)(128)(2,1)S(1)}, bf16[1024]{0:T(1024)(128)(2,1)S(1)}, bf16[1024]{0:T(1024)(128)(2,1)S...) all-reduce(bf16[1024]{0:T(1024)(128)(2,1)S(1)} %dynamic-update-slic, ...), channel_id=1, replica_groups=mesh['batch'=2,'seq'=16] {'seq'}, use_global_device_ids=true, to_apply=%add.1 | all-reduce | flops 8192 | bytes 32768
  87.8 3.9 fusion.91
  94.9 17.4 %all-gather = bf16[16,1,256]{2,1,0:T(2,128)(2,1)S(1)} all-gather(bf16[1,1,256]{2,1,0:T(2,128)(2,1)S(1)} %reshape.468), channel_id=1, replica_groups=mesh['batch'=2,'seq'=16] {'seq'}, dimensions={0}, use_global_device_ids=true | all-gather | bytes 8704 | tf_op jit(solution)/shard_map/all_gather | solution.py:126
  113.7 37.9 %all-gather.18.cloned.1.call-done = bf16[4096,1024]{1,0:T(8,128)(2,1)} async-done(((bf16[256,1024]{1,0:T(8,128)(2,1)}), bf16[4096,1024]{1,0:T(8,128)(2,1)}) %all-gather.18.cloned.1.call-update) | async-done | bytes 8388624 | tf_op jit(solution)/shard_map/all_gather | solution.py:127
  151.7 7.5 fusion.106
  159.2 44.0 %all-gather.10.cloned.1.call-done = bf16[1024,2,1024]{2,1,0:T(2,128)(2,1)} async-done(((bf16[64,2,1024]{2,1,0:T(2,128)(2,1)}), bf16[1024,2,1024]{2,1,0:T(2,128)(2,1)}) %all-gather.10.cloned.1.call-update) | async-done | bytes 4194320 | tf_op jit(solution)/shard_map/all_gather | solution.py:178
  203.3 11.2 copy.135
  214.5 40.6 %all-gather.12.cloned.1.call-done = bf16[1024,2,1024]{2,1,0:T(2,128)(2,1)} async-done(((bf16[64,2,1024]{2,1,0:T(2,128)(2,1)}), bf16[1024,2,1024]{2,1,0:T(2,128)(2,1)}) %all-gather.12.cloned.1.call-update) | async-done | bytes 4194320 | tf_op jit(solution)/shard_map/all_gather | solution.py:179
  255.1 11.2 copy.137
  266.3 6.9 while.78
  267.8 3.8 conditional.15
  267.8 2.4 fusion.10
  270.3 1.3 select_reduce_fusion
  273.3 7.1 while.79
  274.9 3.7 conditional.16
  274.9 3.7 fusion.18
  281.3 15.8 %all-gather.14.cloned.1.call-done = bf16[1024,1024]{1,0:T(8,128)(2,1)} async-done(((bf16[64,1024]{1,0:T(8,128)(2,1)}), bf16[1024,1024]{1,0:T(8,128)(2,1)}) %all-gather.14.cloned.1.call-update) | async-done | bytes 2097168 | tf_op jit(solution)/shard_map/all_gather | solution.py:121
  297.1 2.1 fusion.105
  299.5 73.3 %all-gather.16.cloned.1.call-done = bf16[1024,4096]{1,0:T(8,128)(2,1)} async-done(((bf16[64,4096]{1,0:T(8,128)(2,1)}), bf16[1024,4096]{1,0:T(8,128)(2,1)}) %all-gather.16.cloned.1.call-update) | async-done | bytes 8388624 | tf_op jit(solution)/shard_map/all_gather | solution.py:125
  372.8 9.0 convert_reduce_fusion
  381.8 3.6 multiply_reduce_fusion.1
  389.3 7.8 while.80
  390.8 4.6 conditional.17
  390.9 2.4 fusion.29
  393.7 1.7 fusion.27
  397.8 76.8 %while.82 = (s32[]{:T(128)}, f32[2,512,2,2048]{3,1,0,2:T(8,128)}, s32[64,2]{0,1:T(2,128)S(1)}, s32[2]{0:T(128)S(1)}, s32[1024,2]{0,1:T(2,128)S(1)}, /*index=5*/b...) while((s32[]{:T(128)}, f32[2,512,2,2048]{3,1,0,2:T(8,128)}, ...), condition=%wide.region_36.37_spmd.clone, body=%wide.region_32.36_spmd.clone.sunk | while | flops 550732352 | bytes 76851512 | solution.py:336
  401.1 17.5 %conditional.19 = (f32[512,2,1024]{0,2,1:T(8,128)}, f32[512,2,1024]{0,2,1:T(8,128)}) conditional(s32[]{:T(128)} %convert_element_type.261, () %tuple.279, (pred[2,1,64,512]{3,2,0,1:T(8,128)(4,1)S(1)}, bf16[1024,2,16,64]{0,3,2,1:T(8,128)(2,1)}, s32[]{:T(128)}, bf16[64,2,16,64]{0,3,2,1:T(8,128)(2,1)S(1)}, f32[2,16,64]{2,1,0:T(8,128)S(1)}, ...), branch_computations={%region_34.34_spmd, %region_35.35_spmd} | conditional | flops 548405248 | bytes 26371088 | solution.py:93
  401.1 4.7 fusion.64
  405.8 7.7 convolution_multiply_fusion
  413.6 5.0 fusion.54
  418.6 7.7 maximum_bitcast_fusion.2
  426.3 8.7 copy.172
  435.0 7.8 constant_dynamic-update-slice_fusion.5
  445.6 5.0 conditional.19
  445.6 2.5 reshape.419.clone
  448.1 2.5 reshape.419
  450.6 7.7 maximum_bitcast_fusion.2
  458.3 8.7 copy.172
  467.0 7.7 constant_dynamic-update-slice_fusion.5
  475.7 2.7 fusion.107
  478.5 8.1 fusion.93
  488.1 8.7 fusion.92
  497.9 14.9 %while.81 = (s32[]{:T(128)}, f32[64,2,16,64]{3,0,2,1:T(8,128)S(1)}, s32[64,2]{0,1:T(2,128)S(1)}, s32[1024,2]{0,1:T(2,128)S(1)}, bf16[1024,2,16,64]{0,3,2,1:T(8,1...) while((s32[]{:T(128)}, f32[64,2,16,64]{3,0,2,1:T(8,128)S(1)}, ...), condition=%wide.region_31.32_spmd.clone, body=%wide.region_27.31_spmd.clone.sunk | while | flops 409305664 | bytes 16485149 | solution.py:309
  499.4 11.7 conditional.18
  499.4 4.9 fusion.37
  504.4 6.8 fusion.42
  513.7 154.8 %reduce-scatter.6.cloned.1.call-done = f32[64,2,2048]{2,0,1:T(8,128)} async-done(((f32[1024,2,2048]{2,0,1:T(8,128)}), f32[64,2,2048]{2,0,1:T(8,128)}) %reduce-scatter.6.cloned.1.call-update) | async-done | bytes 1048592 | tf_op jit(solution)/shard_map/reduce_scatter | solution.py:337
  668.5 1.1 slice.37
  670.0 1.1 convert_reduce_fusion.4
  671.6 6.4 fusion.90
  678.3 65.5 %reduce-scatter.10.cloned.1.call-done = f32[64,1024]{1,0:T(8,128)} async-done(((f32[1024,1024]{1,0:T(8,128)}), f32[64,1024]{1,0:T(8,128)}) %reduce-scatter.10.cloned.1.call-update) | async-done | bytes 262160 | tf_op jit(solution)/shard_map/reduce_scatter | solution.py:357
  743.8 182.3 %reduce-scatter.14.cloned.1.call-done = f32[256,1024]{1,0:T(8,128)} async-done(((f32[4096,1024]{1,0:T(8,128)}), f32[256,1024]{1,0:T(8,128)}) %reduce-scatter.14.cloned.1.call-update) | async-done | bytes 1048592 | tf_op jit(solution)/shard_map/reduce_scatter | solution.py:256
  926.1 182.1 %reduce-scatter.12.cloned.1.call-done = f32[64,4096]{1,0:T(8,128)} async-done(((f32[1024,4096]{1,0:T(8,128)}), f32[64,4096]{1,0:T(8,128)}) %reduce-scatter.12.cloned.1.call-update) | async-done | bytes 1048592 | tf_op jit(solution)/shard_map/reduce_scatter | solution.py:254
  1108.2 138.4 %reduce-scatter.8.cloned.1.call-done = f32[64,3072]{1,0:T(8,128)} async-done(((f32[1024,3072]{1,0:T(8,128)}), f32[64,3072]{1,0:T(8,128)}) %reduce-scatter.8.cloned.1.call-update) | async-done | bytes 786448 | tf_op jit(solution)/shard_map/reduce_scatter | solution.py:354
  1248.2 5.6 fusion.84
  1254.7 5.3 multiply_reduce_fusion.2
  1260.5 1.1 reshape.443
  1261.6 60.8 %all-reduce.17 = (f32[1024]{0:T(1024)S(1)}, f32[1024]{0:T(1024)S(1)}, f32[1024]{0:T(1024)S(1)}, f32[1024]{0:T(1024)S(1)}, f32[1024]{0:T(1024)S(1)}, /*index=5*/f...) all-reduce(f32[1024]{0:T(1024)S(1)} %get-tuple-element.1470, ...), channel_id=3, replica_groups=mesh['batch'=2,'seq'=16] {'seq'}, use_global_device_ids=true, to_apply=%region_41.42.clone | all-reduce | flops 12288 | bytes 98304
  1323.0 5.7 all-reduce.18
  1328.7 6.0 all-reduce.23.cloned.1.call-done
  1334.7 2.2 copy.235
  1336.9 1.7 copy.236
  1338.6 2.3 copy.237
  (289 shorter events, 43.6 us)
Async XLA Ops:
  7.2 78.2 %copy-start.27 = (bf16[64,2,1024]{2,1,0:T(2,128)(2,1)S(1)}, bf16[64,2,1024]{2,1,0:T(2,128)(2,1)}, u32[]{:S(2)}) copy-start(bf16[64,2,1024]{2,1,0:T(2,128)(2,1)} %param.37) | copy-start | bytes 786436
  7.2 80.1 %all-gather.8.cloned.1.call-start = ((), (), s32[]{:S(2)}) async-start(), calls=%async_computation.5 | async-start | bytes 6684672 | tf_op jit(solution)/shard_map/all_gather | solution.py:118
  7.9 143.8 %all-gather.18.cloned.1.call-start = ((), (), s32[]{:S(2)}) async-start(), calls=%async_computation.10 | async-start | bytes 8912896 | tf_op jit(solution)/shard_map/all_gather | solution.py:127
  8.7 194.6 %all-gather.10.cloned.1.call-start = ((), (), s32[]{:S(2)}) async-start(), calls=%async_computation.6 | async-start | bytes 4456448 | tf_op jit(solution)/shard_map/all_gather | solution.py:178
  82.8 4.5 copy-start.25
  82.9 4.5 copy-start.23
  86.6 210.5 %copy-start.1 = (f32[128,1024]{1,0:T(8,128)}, f32[128,1024]{1,0:T(8,128)S(1)}, u32[]{:S(2)}) copy-start(f32[128,1024]{1,0:T(8,128)S(1)} %reshape.434) | copy-start | bytes 1572868
  87.1 4.6 copy-start.47
  87.2 0.5 copy-start.34
  87.3 0.5 copy-start.32
  91.7 3.1 copy-start.49
  91.7 20.6 %copy-start.19 = (bf16[64,2,1024]{2,1,0:T(2,128)(2,1)S(1)}, bf16[64,2,1024]{2,1,0:T(2,128)(2,1)}, u32[]{:S(2)}) copy-start(bf16[64,2,1024]{2,1,0:T(2,128)(2,1)} %param.38) | copy-start | bytes 786436
  92.6 162.5 %all-gather.12.cloned.1.call-start = ((), (), s32[]{:S(2)}) async-start(), calls=%async_computation.7 | async-start | bytes 4456448 | tf_op jit(solution)/shard_map/all_gather | solution.py:179
  93.6 203.5 %all-gather.14.cloned.1.call-start = ((), (), s32[]{:S(2)}) async-start(), calls=%async_computation.8 | async-start | bytes 2228224 | tf_op jit(solution)/shard_map/all_gather | solution.py:121
  94.2 278.6 %all-gather.16.cloned.1.call-start = ((), (), s32[]{:S(2)}) async-start(), calls=%async_computation.9 | async-start | bytes 8912896 | tf_op jit(solution)/shard_map/all_gather | solution.py:125
  94.8 573.8 %reduce-scatter.6.cloned.1.call-start = ((), (), s32[]{:S(2)}) async-start(), calls=%async_computation.11 | async-start | bytes 17825792 | tf_op jit(solution)/shard_map/reduce_scatter | solution.py:337
  94.9 290.6 %copy-start.28 = (f32[1024]{0:T(1024)}, f32[1024]{0:T(1024)S(1)}, u32[]{:S(2)}) copy-start(f32[1024]{0:T(1024)S(1)} %convert_element_type.176) | copy-start | bytes 12292
  94.9 277.9 %copy-start.30 = (f32[1024]{0:T(1024)}, f32[1024]{0:T(1024)S(1)}, u32[]{:S(2)}) copy-start(f32[1024]{0:T(1024)S(1)} %convert_element_type.177) | copy-start | bytes 12292
  112.5 273.3 %copy-start.7 = (bf16[128,1024]{1,0:T(8,128)(2,1)}, bf16[128,1024]{1,0:T(8,128)(2,1)S(1)}, u32[]{:S(2)}) copy-start(bf16[128,1024]{1,0:T(8,128)(2,1)S(1)} %reshape.440) | copy-start | bytes 786436
  281.3 100.6 %copy-start.14 = (bf16[128,1024]{1,0:T(8,128)(2,1)}, bf16[128,1024]{1,0:T(8,128)(2,1)S(1)}, u32[]{:S(2)}) copy-start(bf16[128,1024]{1,0:T(8,128)(2,1)S(1)} %convert_element_type.174) | copy-start | bytes 786436
  299.2 86.2 %copy-start.3 = (f32[128,1024]{1,0:T(8,128)}, f32[128,1024]{1,0:T(8,128)S(1)}, u32[]{:S(2)}) copy-start(f32[128,1024]{1,0:T(8,128)S(1)} %get-tuple-element.1639) | copy-start | bytes 1572868
  299.2 86.2 %copy-start.40 = (f32[128]{0:T(128)}, f32[128]{0:T(128)S(1)}, u32[]{:S(2)}) copy-start(f32[128]{0:T(128)S(1)} %broadcast_multiply_fusion.1) | copy-start | bytes 1540
  299.5 86.0 %copy-start.42 = (f32[128]{0:T(128)}, f32[128]{0:T(128)S(1)}, u32[]{:S(2)}) copy-start(f32[128]{0:T(128)S(1)} %fusion.89) | copy-start | bytes 1540
  372.8 9.0 copy-start.6
  381.8 3.6 copy-start.11
  381.8 5.4 copy-start.5
  385.7 2.7 copy-start.9
  385.7 2.9 copy-start.44
  386.5 0.7 copy-start.16
  390.9 2.8 copy-start
  397.0 0.8 copy-start.21
  474.7 0.9 copy-start.15
  474.7 1.0 copy-start.17
  474.7 3.8 copy-start.8
  474.7 3.8 copy-start.13
  474.7 269.1 %reduce-scatter.10.cloned.1.call-start = ((), (), s32[]{:S(2)}) async-start(), calls=%async_computation.13 | async-start | bytes 4456448 | tf_op jit(solution)/shard_map/reduce_scatter | solution.py:357
  478.5 447.6 %reduce-scatter.14.cloned.1.call-start = ((), (), s32[]{:S(2)}) async-start(), calls=%async_computation.15 | async-start | bytes 17825792 | tf_op jit(solution)/shard_map/reduce_scatter | solution.py:256
  486.7 1.0 copy-start.4
  486.7 1.4 copy-start.12
  486.7 1.4 copy-start.29
  486.7 1.4 copy-start.31
  486.7 1.4 copy-start.41
  486.7 1.4 copy-start.43
  486.7 621.5 %reduce-scatter.12.cloned.1.call-start = ((), (), s32[]{:S(2)}) async-start(), calls=%async_computation.14 | async-start | bytes 17825792 | tf_op jit(solution)/shard_map/reduce_scatter | solution.py:254
  496.8 1.1 copy-start.22
  496.8 749.8 %reduce-scatter.8.cloned.1.call-start = ((), (), s32[]{:S(2)}) async-start(), calls=%async_computation.12 | async-start | bytes 13369344 | tf_op jit(solution)/shard_map/reduce_scatter | solution.py:354
  512.8 158.8 %copy-start.2 = (f32[128,1024]{1,0:T(8,128)S(1)}, f32[128,1024]{1,0:T(8,128)}, u32[]{:S(2)}) copy-start(f32[128,1024]{1,0:T(8,128)} %copy-done.1) | copy-start | bytes 1572868
  512.8 158.8 %copy-start.24 = (f32[1024]{0:T(1024)S(1)}, f32[1024]{0:T(1024)}, u32[]{:S(2)}) copy-start(f32[1024]{0:T(1024)} %copy-done.23) | copy-start | bytes 12292
  512.8 158.8 %copy-start.26 = (f32[1024]{0:T(1024)S(1)}, f32[1024]{0:T(1024)}, u32[]{:S(2)}) copy-start(f32[1024]{0:T(1024)} %copy-done.25) | copy-start | bytes 12292
  512.8 158.8 %copy-start.33 = (f32[128]{0:T(128)S(1)}, f32[128]{0:T(128)}, u32[]{:S(2)}) copy-start(f32[128]{0:T(128)} %copy-done.32) | copy-start | bytes 1540
  512.8 158.8 %copy-start.35 = (f32[128]{0:T(128)S(1)}, f32[128]{0:T(128)}, u32[]{:S(2)}) copy-start(f32[128]{0:T(128)} %copy-done.34) | copy-start | bytes 1540
  678.0 569.9 %copy-start.46 = (bf16[1024]{0:T(1024)(128)(2,1)S(1)}, bf16[1024]{0:T(1024)(128)(2,1)}, u32[]{:S(2)}) copy-start(bf16[1024]{0:T(1024)(128)(2,1)} %get-tuple-element.1603) | copy-start | bytes 6148
  678.0 569.9 %copy-start.20 = (bf16[64,2,1024]{2,1,0:T(2,128)(2,1)S(1)}, bf16[64,2,1024]{2,1,0:T(2,128)(2,1)}, u32[]{:S(2)}) copy-start(bf16[64,2,1024]{2,1,0:T(2,128)(2,1)} %param.38) | copy-start | bytes 786436
  678.1 656.7 %all-reduce.23.cloned.1.call-start = ((), (), s32[]{:S(2)}) async-start(), calls=%async_computation.16 | async-start | bytes 6291456 | tf_op jit(solution)/shard_map/psum | solution.py:362
  1254.6 5.4 copy-start.48
  1254.6 5.6 copy-start.10
  1254.6 5.6 copy-start.45
  1259.9 1.7 copy-start.36
  1259.9 1.6 copy-start.37
  1259.9 1.6 copy-start.38
  1259.9 1.6 copy-start.39
  1334.7 6.1 copy-start.18
Sparse Core Ops, SparseCore 0:
  10.3 65.5 all-gather.7
  78.0 73.6 all-gather.17
  154.4 48.7 all-gather.9
  205.9 49.2 all-gather.11
  257.1 39.9 all-gather.13
  299.1 73.6 all-gather.15
  474.8 193.6 reduce-scatter.5
  672.4 71.4 reduce-scatter.9
  748.5 177.5 reduce-scatter.13
  930.6 177.5 reduce-scatter.11
  1112.8 133.7 reduce-scatter.7
  1249.1 85.6 all-reduce.22
where the time goes:
time: 1360 us; the launch traced here: 1350 us
  waiting for transfers between devices  943 us (69%)
  blocking collectives  148 us (11%)
  matrix products  103 us (8%)
  local copies, waits for them, and re-layouts  94.4 us (7%)
  other arithmetic  32.4 us (2%)
  between operations  17.4 us (1%)
    reduce_scatter x1, waiting for transfers between devices, on_device(): lax.psum_scatter(shrink_grad, 'seq', scatter_dimension=0, tiled=True)  182 us
    reduce_scatter x1, waiting for transfers between devices, on_device(): lax.psum_scatter(expand_grad, 'seq', scatter_dimension=0, tiled=True)  182 us
    reduce_scatter x1, waiting for transfers between devices, on_device(): lax.psum_scatter(parts.reshape(count, rows, 2 * width), 'seq', scatter_di...  155 us
    reduce_scatter x1, waiting for transfers between devices, on_device(): lax.psum_scatter(inward_grad, 'seq', scatter_dimension=0, tiled=True)  138 us
    unnamed x2, blocking collectives  125 us
    all_gather x1, waiting for transfers between devices, on_device(): lax.all_gather(expand_weight, 'seq', axis=0, tiled=True)  73.3 us
    reduce_scatter x1, waiting for transfers between devices, on_device(): lax.psum_scatter(outward_grad, 'seq', scatter_dimension=0, tiled=True)  65.5 us
    all_gather x1, waiting for transfers between devices, on_device(): lax.all_gather(key_rows.reshape(local_len, rows, width), 'seq', axis=0, t...  44 us
  transfers between devices with their start and end apart: 12, of which 11 were waited for; matrix products, arithmetic and copies ran while one was open for 9% of the time, Pallas kernels for 0%

commit v1 on v0

v1 whole, which is shorter than its diff:
```python
import functools
import math

import jax
import jax.numpy as jnp
from jax import lax
from jax.experimental import pallas as pl
from jax.experimental.pallas import tpu as pltpu
from jax.sharding import Mesh, PartitionSpec as P


HEADS = 16
NZ = 4
NORM_EPS = 1e-05
NEG = -1e30
F32 = jnp.float32
BF16 = jnp.bfloat16
LAYER_OF_ROW = (1, 2, 0, 3)
SWAP = [(0, 1), (1, 0)]
LAYER = ("x", "y", "c")


def xor_perm(count, k):
    return [(i, i ^ k) for i in range(count)]


def hop(value, axis, count=2, k=1):
    return lax.ppermute(value, axis, xor_perm(count, k))


def pick(value, index, axis=0):
    return lax.dynamic_index_in_dim(value, index, axis, keepdims=False)


def stack_rows(parts):
    return jnp.concatenate(parts, axis=0)


def to_layer(block, ny):
    half = block.shape[0] // 2
    over_x = hop(block, "x")
    over_y = {k: hop(block, "y", ny, k) for k in range(1, ny)}
    mine_c = hop(block, "c")
    over_xy = {
        k: stack_rows([hop(over_x[:half], "y", ny, k), hop(over_y[k][half:], "x")]) for k in range(1, ny)
    }
    near = {(0, 0): block, (1, 0): over_x}
    for k in range(1, ny):
        near[0, k] = over_y[k]
        near[1, k] = over_xy[k]
    far = {key: hop(value, "c") for key, value in near.items() if key != (0, 0)}
    far[0, 0] = mine_c
    return stack_rows([v for dx in range(2) for k in range(ny) for v in (near[dx, k], far[dx, k])])


def from_layer(parts, ny):
    rows, width = parts.shape
    size = rows // (4 * ny)
    view = parts.reshape(2, ny, 2, size, width)
    half = size // 2
    total = {}
    for dx in (1, 0):
        for k in reversed(range(ny)):
            total[dx, k] = view[dx, k, 0].astype(F32) + hop(view[dx, k, 1], "c").astype(F32)
    top, bottom = {}, total[1, 0][half:]
    for k in range(1, ny):
        low = total[1, k].astype(BF16)
        top[k] = total[0, k][:half] + hop(low[:half], "x").astype(F32)
        bottom = bottom + hop(low[half:], "y", ny, k).astype(F32)
    result = total[0, 0]
    for k in range(1, ny):
        send = stack_rows([top[k].astype(BF16), total[0, k][half:].astype(BF16)])
        result = result + hop(send, "y", ny, k).astype(F32)
    send = stack_rows([total[1, 0][:half].astype(BF16), bottom.astype(BF16)])
    return result + hop(send, "x").astype(F32)


def rehome_flat(x, z, c):
    return (x * NZ + z) * 2 + c


def rehome_perm(k):
    return [
        (rehome_flat(x, z, c), rehome_flat(z >> 1, LAYER_OF_ROW[2 * x + (c ^ k)], z & 1))
        for x in range(2)
        for z in range(NZ)
        for c in range(2)
    ]


def to_home(block, place):
    got = [
        lax.ppermute(jnp.where(place.c == k, block[:, 0], block[:, 1]), ("x", "z", "c"), rehome_perm(k))
        for k in range(2)
    ]
    first = place.z < 2
    return stack_rows([jnp.where(first, got[0], got[1]), jnp.where(first, got[1], got[0])])


def to_origin(block, place):
    half = block.shape[0] // 2
    first = place.z < 2
    low, high = block[:half], block[half:]
    sent = [jnp.where(first, low, high), jnp.where(first, high, low)]
    got = [
        lax.ppermute(sent[k], ("x", "z", "c"), [(b, a) for a, b in rehome_perm(k)]) for k in range(2)
    ]
    return jnp.stack(
        [jnp.where(place.c == 0, got[0], got[1]), jnp.where(place.c == 0, got[1], got[0])], axis=1
    )


def over_z(value):
    return [value] + [hop(value, "z", NZ, k) for k in range(1, NZ)]


def sum_over_z(parts):
    total = parts[0].astype(F32)
    for k in range(1, NZ):
        total = total + hop(parts[k].astype(BF16), "z", NZ, k).astype(F32)
    return total


def z_order(value, z):
    quarter = value.shape[1] // NZ
    return jnp.concatenate(
        [lax.dynamic_slice_in_dim(value, (z ^ k) * quarter, quarter, 1) for k in range(NZ)], axis=1
    )


def by_half(x, mine, other, axis):
    return jnp.concatenate([jnp.where(x == 0, mine, other), jnp.where(x == 0, other, mine)], axis=axis)


def sin_cos(position, width):
    feature = jnp.arange(width, dtype=jnp.int32)
    rates = jnp.exp((feature // 2).astype(F32) * (-2.0 * math.log(10000.0) / width))
    angle = position.astype(F32)[:, None] * rates[None, :]
    turn = jnp.round(angle * (2.0 / math.pi))
    rest = angle - turn * 1.5703125
    rest = rest - turn * 0.00048375129699707031
    rest = rest - turn * 7.5497899548918861e-08
    quadrant = turn.astype(jnp.int32) + (feature % 2)[None, :]
    square = rest * rest
    sine = rest + rest * square * (
        -0.16666666641626524 + square * (0.008333329385889463 + square * (-0.00019839334836096632 + square * 2.718311493989822e-06))
    )
    cosine = 1.0 + square * (
        -0.49999999725103100 + square * (0.04166662332373906 + square * (-0.001388676377460993 + square * 2.439044879627741e-05))
    )
    value = jnp.where((quadrant & 1) == 0, sine, cosine)
    return jnp.where((quadrant & 2) == 0, value, -value)


def normalize(values):
    center = values - jnp.mean(values, axis=-1, keepdims=True)
    scale = lax.rsqrt(jnp.mean(center * center, axis=-1, keepdims=True) + NORM_EPS)
    return center * scale, scale


def normalize_back(normal, scale, gain, upstream):
    scaled = upstream * gain
    inner = scaled - jnp.mean(scaled, axis=-1, keepdims=True)
    inner = inner - normal * jnp.mean(scaled * normal, axis=-1, keepdims=True)
    return inner * scale, jnp.sum(upstream * normal, axis=0), jnp.sum(upstream, axis=0)


def dot_nt(a, b):
    return lax.dot_general(a, b, (((1,), (1,)), ((), ())), preferred_element_type=F32)


def dot_tn(a, b):
    return lax.dot_general(a, b, (((0,), (0,)), ((), ())), preferred_element_type=F32)


def dot_nn(a, b):
    return jnp.dot(a, b, preferred_element_type=F32)


BLOCK = 256


def chunk_owner(chunk, ny):
    outer, y = divmod(chunk, ny)
    return ((outer >> 1) * ny + y) * 2 + (outer & 1)


def lane_parts(heads, width):
    if heads == 1:
        return [None]
    lane = lax.broadcasted_iota(jnp.int32, (1, width), 1)
    return [(lane >= h * (width // heads)) & (lane < (h + 1) * (width // heads)) for h in range(heads)]


def only(value, lanes):
    return value if lanes is None else jnp.where(lanes, value, jnp.zeros_like(value))


def allowed_pairs(start_ref, first, total):
    key = lax.broadcasted_iota(jnp.int32, (total, BLOCK), 0)
    frame = first + lax.broadcasted_iota(jnp.int32, (total, BLOCK), 1)
    return (key >= start_ref[:, first : first + BLOCK]) & (key <= frame)


def attend(heads, ny, size, me_ref, qkv_ref, start_ref, near_ref, far_ref, log_ref, q_s, k_s, vt_s):
    count = 4 * ny
    width = q_s.shape[1]
    me = me_ref[0]
    for chunk in range(count):
        rel = me ^ chunk_owner(chunk, ny)
        rows = pl.ds(pl.multiple_of(rel * size, size), size)
        here = slice(chunk * size, (chunk + 1) * size)
        q_s[here, :] = qkv_ref[rows, 0:width] * 0.125
        k_s[here, :] = qkv_ref[rows, width : 2 * width]
        vt_s[:, here] = jnp.transpose(qkv_ref[rows, 2 * width : 3 * width].astype(F32)).astype(BF16)
    lanes = lane_parts(heads, width)
    each = width // heads
    for block in range(count * size // BLOCK):
        first = block * BLOCK
        total = first + BLOCK
        allowed = allowed_pairs(start_ref, first, total)
        q_block = q_s[first:total, :]
        contexts = []
        for h in range(heads):
            scores = dot_nt(k_s[0:total, :], only(q_block, lanes[h]))
            scores = jnp.where(allowed, scores, NEG)
            top = jnp.max(scores, axis=0, keepdims=True)
            weight = jnp.exp(scores - top)
            mass = jnp.sum(weight, axis=0, keepdims=True)
            part = dot_nn(vt_s[h * each : (h + 1) * each, 0:total], weight.astype(BF16))
            contexts.append(part / mass)
            log_ref[h : h + 1, first:total] = top + jnp.log(mass)
        context = contexts[0] if heads == 1 else jnp.concatenate(contexts, axis=0)
        context = jnp.transpose(context).astype(BF16)
        for sub in range(BLOCK // size):
            owner = chunk_owner(block * (BLOCK // size) + sub, ny)
            piece = context[sub * size : (sub + 1) * size]
            near_ref[owner] = piece
            far_ref[pl.ds(pl.multiple_of((me ^ owner) * size, size), size), :] = piece


def attend_back(
    heads, ny, size, me_ref, qkv_ref, grad_ref, start_ref, log_ref, out_ref, q_s, k_s, v_s, g_s, kt_s, dq_s, dk_s, dv_s
):
    count = 4 * ny
    width = q_s.shape[1]
    me = me_ref[0]
    for chunk in range(count):
        rel = me ^ chunk_owner(chunk, ny)
        rows = pl.ds(pl.multiple_of(rel * size, size), size)
        here = slice(chunk * size, (chunk + 1) * size)
        q_s[here, :] = qkv_ref[rows, 0:width] * 0.125
        key = qkv_ref[rows, width : 2 * width]
        k_s[here, :] = key
        kt_s[:, here] = jnp.transpose(key.astype(F32)).astype(BF16)
        v_s[here, :] = qkv_ref[rows, 2 * width : 3 * width]
        g_s[here, :] = grad_ref[rows, :]
    dk_s[...] = jnp.zeros_like(dk_s)
    dv_s[...] = jnp.zeros_like(dv_s)
    lanes = lane_parts(heads, width)
    each = width // heads
    for block in range(count * size // BLOCK):
        first = block * BLOCK
        total = first + BLOCK
        allowed = allowed_pairs(start_ref, first, total)
        q_block, g_block = q_s[first:total, :], g_s[first:total, :]
        queries = []
        for h in range(heads):
            q_one, g_one = only(q_block, lanes[h]), only(g_block, lanes[h])
            scores = dot_nt(k_s[0:total, :], q_one)
            probs = jnp.where(allowed, jnp.exp(scores - log_ref[h : h + 1, first:total]), 0.0)
            prob_grad = dot_nt(v_s[0:total, :], g_one)
            delta = jnp.sum(probs * prob_grad, axis=0, keepdims=True)
            score_grad = (probs * (prob_grad - delta)).astype(BF16)
            dv_s[0:total, :] += dot_nn(probs.astype(BF16), g_one)
            dk_s[0:total, :] += dot_nn(score_grad, q_one)
            queries.append(dot_nn(kt_s[h * each : (h + 1) * each, 0:total], score_grad))
        query_grad = queries[0] if heads == 1 else jnp.concatenate(queries, axis=0)
        dq_s[first:total, :] = jnp.transpose(query_grad) * 0.125
    for chunk in range(count):
        rel = me ^ chunk_owner(chunk, ny)
        rows = pl.ds(pl.multiple_of(rel * size, size), size)
        here = slice(chunk * size, (chunk + 1) * size)
        out_ref[rows, 0:width] = dq_s[here, :].astype(BF16)
        out_ref[rows, width : 2 * width] = dk_s[here, :].astype(BF16)
        out_ref[rows, 2 * width : 3 * width] = dv_s[here, :].astype(BF16)


def whole(count):
    return [pl.BlockSpec(memory_space=pltpu.VMEM)] * count


def attention(qkv, starts, me, heads, ny, size):
    frames, wide = qkv.shape
    width = wide // 3
    pairs = frames * frames * heads
    return pl.pallas_call(
        functools.partial(attend, heads, ny, size),
        out_shape=(
            jax.ShapeDtypeStruct((4 * ny, size, width), BF16),
            jax.ShapeDtypeStruct((frames, width), BF16),
            jax.ShapeDtypeStruct((heads, frames), F32),
        ),
        in_specs=[pl.BlockSpec(memory_space=pltpu.SMEM)] + whole(2),
        out_specs=tuple(whole(3)),
        scratch_shapes=[
            pltpu.VMEM((frames, width), BF16),
            pltpu.VMEM((frames, width), BF16),
            pltpu.VMEM((width, frames), BF16),
        ],
        compiler_params=pltpu.CompilerParams(vmem_limit_bytes=40 << 20),
        cost_estimate=pl.CostEstimate(flops=pairs * 256, bytes_accessed=frames * wide * 4, transcendentals=pairs // 2),
        name="attend",
    )(me, qkv, starts)


def attention_back(qkv, grad, starts, log_total, me, heads, ny, size):
    frames, wide = qkv.shape
    width = wide // 3
    pairs = frames * frames * heads
    return pl.pallas_call(
        functools.partial(attend_back, heads, ny, size),
        out_shape=jax.ShapeDtypeStruct((frames, wide), BF16),
        in_specs=[pl.BlockSpec(memory_space=pltpu.SMEM)] + whole(4),
        out_specs=whole(1)[0],
        scratch_shapes=[pltpu.VMEM((frames, width), BF16)] * 4
        + [pltpu.VMEM((width, frames), BF16)]
        + [pltpu.VMEM((frames, width), F32)] * 3,
        compiler_params=pltpu.CompilerParams(vmem_limit_bytes=40 << 20),
        cost_estimate=pl.CostEstimate(flops=pairs * 640, bytes_accessed=frames * wide * 6, transcendentals=pairs // 2),
        name="attend_back",
    )(me, qkv, grad, starts, log_total)


class Place:
    def __init__(self):
        self.x, self.z, self.y, self.c = (lax.axis_index(a) for a in ("x", "z", "y", "c"))


def on_device(
    groups,
    ny,
    frames,
    cotangent,
    segment_lengths,
    position_offsets,
    first_gain,
    first_shift,
    inward_weight,
    query_bias,
    value_bias,
    outward_weight,
    outward_bias,
    second_gain,
    second_shift,
    expand_weight,
    expand_bias,
    shrink_weight,
    shrink_bias,
):
    place = Place()
    x, z, y, c = place.x, place.z, place.y, place.c
    local_len, rows, width = frames.shape
    share = inward_weight.shape[0]
    layer = 4 * ny
    full_len = local_len * NZ * ny * 2
    size = 2 * local_len
    hd = HEADS // layer
    head_dim = width // HEADS
    hw = hd * head_dim
    hidden = expand_bias.shape[0]
    part = hidden // 2
    me = (x * ny + y) * 2 + c

    def sum_groups(value):
        return lax.psum(value, "g") if groups > 1 else value

    fr = to_home(frames, place)
    ct = to_home(cotangent, place)

    table = jnp.stack([segment_lengths, position_offsets], axis=1)
    other = hop(table, "x")
    row_x = jnp.where((z == 0) | (z == 3), 1, 0)
    table = pick(jnp.where(x == row_x, table, other), z >> 1)
    lengths, offsets = table[0], table[1]
    count = lengths.shape[0]
    starts = jnp.sum(
        jnp.where(jnp.arange(count)[None, :] < jnp.arange(count)[:, None], lengths[None, :], 0), axis=1
    )
    frame_ids = jnp.arange(full_len, dtype=jnp.int32)
    row_starts = jnp.max(jnp.where(starts[:, None] <= frame_ids[None, :], starts[:, None], 0), axis=0)[None, :]
    chunk = (2 * x + c) * ny + y
    mine = chunk * size + jnp.arange(size, dtype=jnp.int32)
    inside = (mine[:, None] >= starts[None, :]) & (mine[:, None] < (starts + lengths)[None, :])
    position = jnp.sum(jnp.where(inside, offsets[None, :] + mine[:, None] - starts[None, :], 0), axis=1)

    small = [first_gain, first_shift, query_bias, value_bias, outward_bias, second_gain, second_shift, shrink_bias]
    packed = jnp.stack(small + [jnp.zeros_like(first_gain)] * (16 - len(small)))
    lines = over_z(packed)
    grid = jnp.stack(lines, axis=0)
    grid = jnp.stack([grid] + [hop(grid, "y", ny, k) for k in range(1, ny)], axis=1)
    grid = jnp.stack([grid, hop(grid, "c")], axis=2)
    ids = jnp.arange(NZ * ny * 2)
    mine_id = (z * ny + y) * 2 + c
    select = (ids[:, None] == (ids[None, :] ^ mine_id)).astype(BF16)
    vectors = dot_nn(select, grid.reshape(NZ * ny * 2, 16 * share)).reshape(NZ * ny * 2, 16, share)
    vectors = jnp.swapaxes(vectors, 0, 1).reshape(16, width)
    gain_one, shift_one, query_b, value_b, outward_b, gain_two, shift_two, shrink_b = (
        vectors[i][None, :] for i in range(8)
    )
    expand_line = over_z(jnp.where(x == 0, expand_bias[:part], expand_bias[part:]))
    expand_b = jnp.concatenate(expand_line).astype(F32)[None, :]

    def my_heads(value):
        return pick(pick(pick(value.reshape(2, hd, ny, 2, head_dim), x), y, 1), c, 1).reshape(1, hw)

    qkv_bias = jnp.concatenate([my_heads(query_b), jnp.zeros((1, hw), F32), my_heads(value_b)], axis=1)

    in_cols = pick(inward_weight.reshape(share, 3, 2, hd, ny, 2, head_dim), x, 2)
    in_cols = jnp.transpose(in_cols, (3, 4, 0, 1, 2, 5)).reshape(ny * 2, share, 3 * hw)
    ex_cols = pick(expand_weight.reshape(share, NZ, ny, 2, 2, part), x, 4)
    ex_cols = jnp.stack([pick(ex_cols, z ^ m, 1) for m in range(NZ)], axis=3)
    ex_cols = jnp.transpose(ex_cols, (1, 2, 0, 3, 4)).reshape(ny * 2, share, NZ * part)
    quarter = lax.all_to_all(jnp.concatenate([in_cols, ex_cols], axis=2), ("y", "c"), 0, 0, tiled=True)
    quarter = quarter.reshape(ny * 2 * share, 3 * hw + NZ * part)
    w_in = stack_rows(over_z(quarter[:, : 3 * hw]))
    outward = lax.all_gather(outward_weight, ("z", "y", "c"), axis=0, tiled=True)
    ex_parts = over_z(quarter[:, 3 * hw :])
    w_expand = stack_rows(
        [
            jnp.concatenate([got[:, (q ^ k) * part : ((q ^ k) + 1) * part] for k in range(NZ)], axis=1)
            for q, got in enumerate(ex_parts)
        ]
    )
    w_shrink = stack_rows(over_z(lax.dynamic_slice_in_dim(shrink_weight, x * part, part, 0)))
    w_out = outward.reshape(2, hd, ny, 2, head_dim, width)
    w_out = pick(pick(pick(w_out, x), y, 1), c, 1).reshape(hw, width)

    inputs = fr.astype(F32) + sin_cos(position, width)
    normal_one, scale_one = normalize(inputs)
    first = (normal_one * gain_one + shift_one).astype(BF16)
    first_all = to_layer(z_order(first, z), ny)
    qkv = (dot_nn(first_all, w_in) + qkv_bias).astype(BF16)
    me_ref = jnp.reshape(me, (1,)).astype(jnp.int32)
    context_to, context_all, log_total = attention(qkv, row_starts, me_ref, hd, ny, size)
    context = lax.all_to_all(context_to, LAYER, 0, 0, tiled=True)
    context = jnp.transpose(context.reshape(2, ny, 2, size, hd, head_dim), (3, 0, 4, 1, 2, 5)).reshape(size, width)
    middle = inputs + dot_nn(context, outward) + outward_b

    upstream_all = to_layer(ct, ny)
    normal_two, scale_two = normalize(middle)
    second = (normal_two * gain_two + shift_two).astype(BF16)
    second_all = to_layer(z_order(second, z), ny)
    before = dot_nn(second_all, w_expand) + expand_b
    active_grad = dot_nt(upstream_all, w_shrink)
    rate = math.sqrt(2.0 / math.pi)
    inner = jnp.tanh(rate * (before + 0.044715 * before * before * before))
    active = (0.5 * before * (1.0 + inner)).astype(BF16)
    slope = 0.5 * (1.0 + inner) + 0.5 * before * (1.0 - inner * inner) * rate * (1.0 + 3 * 0.044715 * before * before)
    before_grad = (active_grad * slope).astype(BF16)
    second_grad = z_order(from_layer(dot_nt(before_grad, w_expand).astype(BF16), ny), z)
    out_part = from_layer(dot_nn(active, w_shrink).astype(BF16), ny)
    layer_output = to_origin((middle + out_part + shrink_b).astype(BF16), place)
    shrink_part = dot_tn(active, upstream_all).astype(BF16)
    expand_part = dot_tn(second_all, before_grad).astype(BF16)
    expand_b_sum = jnp.sum(before_grad.astype(F32), axis=0)

    upstream = ct.astype(F32)
    middle_part, gain_two_sum, shift_two_sum = normalize_back(normal_two, scale_two, gain_two, second_grad)
    middle_grad = upstream + middle_part
    low_middle = middle_grad.astype(BF16)
    low_all = to_layer(low_middle, ny)
    context_grad = dot_nt(low_all, w_out).astype(BF16)
    outward_part = dot_tn(context_all, low_all)
    mixed_grad = attention_back(qkv, context_grad, row_starts, log_total, me_ref, hd, ny, size)
    first_grad = z_order(from_layer(dot_nt(mixed_grad, w_in).astype(BF16), ny), z)
    inward_part = dot_tn(first_all, mixed_grad).astype(BF16)
    input_part, gain_one_sum, shift_one_sum = normalize_back(normal_one, scale_one, gain_one, first_grad)
    frames_grad = to_origin((middle_grad + input_part).astype(BF16), place).astype(F32)

    shrink_sum = sum_groups(sum_over_z([shrink_part[k * part : (k + 1) * part] for k in range(NZ)])).astype(BF16)
    g_shrink = by_half(x, shrink_sum, hop(shrink_sum, "x"), 0).astype(F32)
    rows_z = ny * 2 * share
    expand_sum = sum_over_z(
        [
            jnp.concatenate(
                [expand_part[q * rows_z : (q + 1) * rows_z, (q ^ m) * part : ((q ^ m) + 1) * part] for m in range(NZ)],
                axis=1,
            )
            for q in range(NZ)
        ]
    )
    inward_sum = sum_over_z([inward_part[q * rows_z : (q + 1) * rows_z] for q in range(NZ)])
    both = sum_groups(jnp.concatenate([inward_sum, expand_sum], axis=1)).astype(BF16)
    both = lax.all_to_all(both.reshape(ny * 2, share, -1), ("y", "c"), 0, 0, tiled=True)
    both_x = hop(both, "x")
    in_pair = [v[:, :, : 3 * hw].reshape(ny, 2, share, 3, hd, head_dim) for v in (both, both_x)]
    g_inward = by_half(x, in_pair[0][None], in_pair[1][None], 0)
    g_inward = jnp.transpose(g_inward, (3, 4, 0, 5, 1, 2, 6)).reshape(share, 3 * width).astype(F32)
    ex_pair = [v[:, :, 3 * hw :].reshape(ny, 2, share, NZ, part) for v in (both, both_x)]
    g_expand = by_half(x, ex_pair[0][None], ex_pair[1][None], 0)
    g_expand = jnp.stack([pick(g_expand, z ^ m, 4) for m in range(NZ)], axis=0)
    g_expand = jnp.transpose(g_expand, (4, 0, 2, 3, 1, 5)).reshape(share, -1).astype(F32)

    if share == head_dim and hd == 2:
        half = width // 2
        split = outward_part.astype(BF16).reshape(2, share, 2, half)
        keep, send = pick(split, x, 2), pick(split, 1 - x, 2)
        line = by_half(x, keep, hop(send, "x"), 0)
        out_sum = sum_groups(sum_over_z([pick(line, z ^ k) for k in range(NZ)])).astype(BF16)
        g_outward = by_half(x, out_sum, hop(out_sum, "x"), 1).astype(F32)
    else:
        spot = jnp.zeros((2, ny, 2, hd, head_dim, width), F32)
        spot = lax.dynamic_update_slice(spot, outward_part.reshape(1, 1, 1, hd, head_dim, width), (x, y, c, 0, 0, 0))
        spot = jnp.transpose(spot, (0, 3, 1, 2, 4, 5)).reshape(width, width).astype(BF16)
        g_outward = lax.psum_scatter(spot, ("z", "y", "c"), scatter_dimension=0, tiled=True)
        g_outward = lax.psum(g_outward.astype(F32), ("g", "x"))

    mixed_sum = jnp.sum(mixed_grad.astype(F32), axis=0)

    def from_heads(value):
        spot = jnp.zeros((2, hd, ny, 2, head_dim), F32)
        return lax.dynamic_update_slice(spot, value.reshape(1, hd, 1, 1, head_dim), (x, 0, y, c, 0)).reshape(width)

    flat = [
        gain_one_sum,
        shift_one_sum,
        from_heads(mixed_sum[:hw]),
        from_heads(mixed_sum[2 * hw :]),
        jnp.sum(low_middle.astype(F32), axis=0),
        gain_two_sum,
        shift_two_sum,
        jnp.sum(upstream, axis=0),
    ]
    line = jnp.stack([pick(expand_b_sum.reshape(NZ, part), z ^ m) for m in range(NZ)])
    spot = jnp.zeros((NZ, ny, 2, 2, part), F32)
    spot = lax.dynamic_update_slice(spot, line.reshape(NZ, 1, 1, 1, part), (0, y, c, x, 0))
    sums = jnp.stack(flat).reshape(8, NZ, ny, 2, share)
    sums = jnp.transpose(sums, (1, 2, 3, 0, 4)).reshape(NZ, ny, 2, 8 * share)
    sums = jnp.concatenate([sums, spot.reshape(NZ, ny, 2, hidden)], axis=3)
    sums = pick(sums, c, 2) + hop(pick(sums, 1 - c, 2), "c")
    over = pick(sums, y, 1)
    for k in range(1, ny):
        over = over + hop(pick(sums, y ^ k, 1), "y", ny, k)
    over = over + hop(over, "x")
    total = pick(over, z)
    for k in range(1, NZ):
        total = total + hop(pick(over, z ^ k), "z", NZ, k)
    total = sum_groups(total)
    g_small = total[: 8 * share].reshape(8, share)
    g_expand_b = total[8 * share :]
    return (
        layer_output,
        frames_grad,
        g_small[0],
        g_small[1],
        g_inward,
        g_small[2],
        g_small[3],
        g_outward,
        g_small[4],
        g_small[5],
        g_small[6],
        g_expand,
        g_expand_b,
        g_shrink,
        g_small[7],
    )


def solution(mesh):
    batch, seq = mesh.shape["batch"], mesh.shape["seq"]
    groups, ny = batch // 2, seq // (2 * NZ)
    fine = Mesh(mesh.devices.reshape(groups, 2, NZ, ny, 2), ("g", "x", "z", "y", "c"))
    b, s = ("g", "x"), ("z", "y", "c")
    in_specs = (
        P(s, b, None),
        P(s, b, None),
        P(b, None),
        P(b, None),
        P(s),
        P(s),
        P(s, None),
        P(s),
        P(s),
        P(s, None),
        P(s),
        P(s),
        P(s),
        P(s, None),
        P(s),
        P(s, None),
        P(s),
    )
    out_specs = (
        P(s, b, None),
        P(s, b, None),
        P(s),
        P(s),
        P(s, None),
        P(s),
        P(s),
        P(s, None),
        P(s),
        P(s),
        P(s),
        P(s, None),
        P(s),
        P(s, None),
        P(s),
    )
    return jax.shard_map(
        functools.partial(on_device, groups, ny), mesh=fine, in_specs=in_specs, out_specs=out_specs, check_vma=False
    )
```

time: 1360 us -> 436 us (0.32)
  waiting for transfers between devices: 943 us -> 147 us
  blocking collectives: 148 us -> 0 us
  starting transfers between devices: 0.87 us -> 140 us
  matrix products: 103 us -> 27.6 us
  local copies, waits for them, and re-layouts: 94.4 us -> 58.4 us
    reduce_scatter x5 -> x0, waiting for transfers between devices: 723 us -> none  [the longest x1 182 us: on_device(): lax.psum_scatter(shrink_grad, 'seq', scatter_dimension=0, tiled=True)]
    all_gather x6 -> x1, waiting for transfers between devices: 212 us -> 0.02 us  [on_device(): lax.all_gather(outward_weight, ('z', 'y', 'c'), axis=0, tiled=True)]
    ppermute x0 -> x104, waiting for transfers between devices: none -> 144 us  [the longest x96 133 us: hop(): return lax.ppermute(value, axis, xor_perm(count, k))]
    ppermute x0 -> x104, starting transfers between devices: none -> 129 us  [the longest x96 105 us: hop(): return lax.ppermute(value, axis, xor_perm(count, k))]
    unnamed x2 -> x0, blocking collectives: 125 us -> none
    dot_general x21 -> x13, matrix products: 103 us -> 27.6 us  [the longest x4 11.5 us: dot_nt(): lax.dot_general(a, b, (((1,), (1,)), ((), ())), preferred_element_type=F32)]
    dynamic_update_slice x4 -> x3, local copies, waits for them, and re-layouts: 32.9 us -> 0.5 us  [the longest x1 0.43 us: on_device(): lax.dynamic_update_slice(spot, line.reshape(NZ, 1, 1, 1, part), (0, y, c,...]
    all_gather x2 -> x0, local copies, waits for them, and re-layouts: 22.4 us -> none  [the longest x1 11.2 us: on_device(): lax.all_gather(key_rows.reshape(local_len, rows, width), 'seq', axis=0, t...]
  transfers between devices with their start and end apart: 12 -> 108, of which waited for: 11 -> 41; matrix products, arithmetic and copies ran while one was open for 9% -> 17% of each run, Pallas kernels for 0% -> 1%
where the time goes in v1:
time: 436 us; the launch traced here: 429 us
  waiting for transfers between devices  147 us (34%)
  starting transfers between devices  140 us (32%)
  local copies, waits for them, and re-layouts  58.4 us (13%)
  other arithmetic  29.4 us (7%)
  matrix products  27.6 us (6%)
  between operations  16.6 us (4%)
  Pallas kernels  9.94 us (2%)
    ppermute x96, waiting for transfers between devices, hop(): return lax.ppermute(value, axis, xor_perm(count, k))  133 us
    ppermute x96, starting transfers between devices, hop(): return lax.ppermute(value, axis, xor_perm(count, k))  105 us
    unnamed x175, local copies, waits for them, and re-layouts  25.2 us
    ppermute x4, starting transfers between devices, to_origin(): lax.ppermute(sent[k], ('x', 'z', 'c'), [(b, a) for a, b in rehome_perm(k)])  13.2 us
    ppermute x4, starting transfers between devices, to_home(): lax.ppermute(jnp.where(place.c == k, block[:, 0], block[:, 1]), ('x', 'z'...  11.5 us
    dot_general x4, matrix products, dot_nt(): lax.dot_general(a, b, (((1,), (1,)), ((), ())), preferred_element_type=F32)  11.5 us
    dot_general x4, matrix products, dot_tn(): lax.dot_general(a, b, (((0,), (0,)), ((), ())), preferred_element_type=F32)  8.79 us
  transfers between devices with their start and end apart: 108, of which 41 were waited for; matrix products, arithmetic and copies ran while one was open for 17% of the time, Pallas kernels for 1%

profile of v1, /device:TPU:0, one launch (start us, length us, event | category | flops | bytes accessed | tf_op | source)
XLA Modules:
  0.0 429.1 jit_solution(373473549716024731)
XLA Ops:
  8.0 5.0 %collective-permute-start.32 = (bf16[128]{0:T(256)(128)(2,1)S(1)}, bf16[128]{0:T(256)(128)(2,1)S(1)}, u32[]{:S(2)}, u32[]{:S(2)}) collective-permute-start(bf16[128]{0:T(256)(128)(2,1)S(1)} %broadcast_select_fusion.19), channel_id=1, source_target_pairs={{0,12},{4,8},{8,4},{12,0},{1,13},{5,9},{9,5},{13,1},{2,14},{6,10},... | collective-permute-start | bytes 776 | tf_op jit(solution)/shard_map/ppermute | solution.py:28
  13.9 2.0 collective-permute-start.5
  23.8 3.5 all-to-all-start
  30.8 3.3 collective-permute-start
  34.2 2.0 collective-permute-start.6
  39.2 3.3 collective-permute-start.1
  43.1 2.5 collective-permute-start.47
  47.3 2.4 collective-permute-start.46
  52.5 1.7 collective-permute-start.9
  54.3 3.3 collective-permute-done.46
  57.6 8.0 %collective-permute-start.8 = (bf16[128,1024]{1,0:T(8,128)(2,1)S(1)}, bf16[128,1024]{1,0:T(8,128)(2,1)}, u32[]{:S(2)}, u32[]{:S(2)}) collective-permute-start(bf16[128,1024]{1,0:T(8,128)(2,1)S(1)} %get-tuple-element.206), channel_id=1, source_target_pairs={{0,1},{1,0},{2,3},{3,2},{4,5},{5,4},{6,7},{7,6},{8,9},{9,8},{10,11... | collective-permute-start | bytes 786440 | tf_op jit(solution)/shard_map/ppermute | solution.py:28
  67.6 1.7 collective-permute-start.49
  69.4 2.0 collective-permute-start.51
  74.9 1.9 collective-permute-done.11
  77.8 4.6 %collective-permute-done.51 = bf16[128,1024]{1,0:T(8,128)(2,1)S(1)} collective-permute-done((bf16[128,1024]{1,0:T(8,128)(2,1)}, bf16[128,1024]{1,0:T(8,128)(2,1)S(1)}, u32[]{:S(2)}, u32[]{:S(2)}) %collective-permute-start.51) | collective-permute-done | bytes 262176 | tf_op jit(solution)/shard_map/ppermute | solution.py:28
  86.9 1.9 constant_dynamic-update-slice_fusion.25
  89.5 2.2 collective-permute-start.35
  93.5 2.2 collective-permute-start.29
  98.3 16.1 %collective-permute-done.29 = bf16[256,512]{1,0:T(8,128)(2,1)S(1)} collective-permute-done((bf16[256,512]{1,0:T(8,128)(2,1)S(1)}, bf16[256,512]{1,0:T(8,128)(2,1)S(1)}, u32[]{:S(2)}, u32[]{:S(2)}) %collective-permute-start.29) | collective-permute-done | bytes 262176 | tf_op jit(solution)/shard_map/ppermute | solution.py:28
  117.1 15.0 %collective-permute-start.16 = (bf16[256,384]{1,0:T(8,128)(2,1)S(1)}, bf16[256,384]{1,0:T(8,128)(2,1)S(1)}, u32[]{:S(2)}, u32[]{:S(2)}) collective-permute-start(bf16[256,384]{1,0:T(8,128)(2,1)S(1)} %slice.544), channel_id=1, source_target_pairs={{0,4},{4,0},{8,12},{12,8},{1,5},{5,1},{9,13},{13,9},{2,6},{6,2},{1... | collective-permute-start | bytes 589832 | tf_op jit(solution)/shard_map/ppermute | solution.py:28
  134.5 3.1 collective-permute-done.16
  138.9 4.9 %attend.1 = (bf16[8,128,128]{2,1,0:T(8,128)(2,1)}, bf16[1024,128]{1,0:T(8,128)(2,1)S(1)}, f32[2,1024]{1,0:T(2,128)S(1)}) custom-call(s32[1]{0:T(128)} %bitcast.6.me_ref, bf16[1024,384]{1,0:T(8,128)(2,1)S(1)} %add_convert_fusion.qkv_ref, s32[1,1024]{1,0:T(1,128)S(1)} %bitcast.252), custom_call_target="tpu_custom_call" | custom-call | flops 536870912 | bytes 1572864 | tf_op jit(solution)/shard_map/attend/pallas_call | solution.py:297
  143.8 3.6 all-to-all-start.1
  149.8 3.6 all-to-all-done.1
  153.6 2.1 fusion.108
  159.2 1.9 collective-permute-start.34
  163.1 2.1 collective-permute-done.20
  168.4 1.8 collective-permute-done.25
  170.2 1.7 collective-permute-start.33
  176.1 2.4 convolution_convert_fusion.3
  179.9 3.4 convert_reduce_fusion
  186.3 5.0 %convolution_convert_fusion.1 = bf16[1024,1024]{1,0:T(8,128)(2,1)} fusion(bf16[1024,512]{1,0:T(8,128)(2,1)S(1)} %get-tuple-element.253, bf16[256,128]{1,0:T(8,128)(2,1)S(1)} %copy-done.32, bf16[256,128]{1,0:T(8,128)(2,1)S(1)} %copy-done.33, bf16[256,128]{1,0:T(8,128)(2,1)S(1)} %copy-done.34, bf16[256,128]{1,0:T(8,128)(2,1)S(1)} %copy-done.31, ...), kind=kOutput, calls=%fused_computation.12 | convolution fusion | flops 1086324736 | bytes 4194304 | tf_op jit(solution)/shard_map/dot_general | solution.py:169
  191.4 2.5 convolution_convert_fusion.2
  198.7 2.4 collective-permute-start.93
  208.4 21.2 %collective-permute-done.100 = bf16[128,1024]{1,0:T(8,128)(2,1)S(1)} collective-permute-done((bf16[128,1024]{1,0:T(8,128)(2,1)S(1)}, bf16[128,1024]{1,0:T(8,128)(2,1)S(1)}, u32[]{:S(2)}, u32[]{:S(2)}) %collective-permute-start.100) | collective-permute-done | bytes 262176 | tf_op jit(solution)/shard_map/ppermute | solution.py:28
  229.8 16.9 %collective-permute-done.101 = bf16[128,1024]{1,0:T(8,128)(2,1)S(1)} collective-permute-done((bf16[128,1024]{1,0:T(8,128)(2,1)S(1)}, bf16[128,1024]{1,0:T(8,128)(2,1)S(1)}, u32[]{:S(2)}, u32[]{:S(2)}) %collective-permute-start.101) | collective-permute-done | bytes 262176 | tf_op jit(solution)/shard_map/ppermute | solution.py:28
  251.8 2.6 collective-permute-done.39
  256.5 3.6 collective-permute-done.62
  266.8 6.8 %collective-permute-done.63 = bf16[128,1024]{1,0:T(8,128)(2,1)S(1)} collective-permute-done((bf16[128,1024]{1,0:T(8,128)(2,1)S(1)}, bf16[128,1024]{1,0:T(8,128)(2,1)S(1)}, u32[]{:S(2)}, u32[]{:S(2)}) %collective-permute-start.63) | collective-permute-done | bytes 262176 | tf_op jit(solution)/shard_map/ppermute | solution.py:28
  273.8 2.5 collective-permute-done.40
  298.0 2.9 convolution_convert_fusion.6
  301.6 5.0 %attend_back.1 = bf16[1024,384]{1,0:T(8,128)(2,1)S(1)} custom-call(s32[1]{0:T(128)} %bitcast.6.me_ref, bf16[1024,384]{1,0:T(8,128)(2,1)S(1)} %add_convert_fusion.qkv_ref, bf16[1024,128]{1,0:T(8,128)(2,1)S(1)} %convolution_convert_fusion.7.grad_ref, s32[1,1024]{1,0:T(1,128)S(1)} %bitcast.253, f32[2,1024]{1,0:T(2,128)S(1)} %get-tuple-element.19.log_ref), custom_call_target="tpu_custom_call" | custom-call | flops 1342177280 | bytes 2359296 | tf_op jit(solution)/shard_map/attend_back/pallas_call | solution.py:321
  306.7 2.2 convolution_convert_fusion.5
  310.5 2.4 convolution_convert_fusion
  317.4 2.5 collective-permute-start.97
  320.8 1.9 collective-permute-start.98
  323.6 1.9 collective-permute-done.97
  325.5 2.8 collective-permute-start.44
  328.3 3.6 collective-permute-start.45
  332.1 2.7 collective-permute-start.90
  337.9 9.4 %collective-permute-done.88 = bf16[256,384]{1,0:T(8,128)(2,1)S(1)} collective-permute-done((bf16[256,384]{1,0:T(8,128)(2,1)}, bf16[256,384]{1,0:T(8,128)(2,1)S(1)}, u32[]{:S(2)}, u32[]{:S(2)}) %collective-permute-start.88) | collective-permute-done | bytes 196640 | tf_op jit(solution)/shard_map/ppermute | solution.py:28
  347.3 9.5 %collective-permute-done.89 = bf16[256,384]{1,0:T(8,128)(2,1)S(1)} collective-permute-done((bf16[256,384]{1,0:T(8,128)(2,1)}, bf16[256,384]{1,0:T(8,128)(2,1)S(1)}, u32[]{:S(2)}, u32[]{:S(2)}) %collective-permute-start.89) | collective-permute-done | bytes 196640 | tf_op jit(solution)/shard_map/ppermute | solution.py:28
  359.7 3.5 all-to-all-start.2
  364.3 4.9 %collective-permute-done.75 = bf16[64,1024]{1,0:T(8,128)(2,1)S(1)} collective-permute-done((bf16[64,1024]{1,0:T(8,128)(2,1)S(1)}, bf16[64,1024]{1,0:T(8,128)(2,1)S(1)}, u32[]{:S(2)}, u32[]{:S(2)}) %collective-permute-start.75) | collective-permute-done | bytes 131104 | tf_op jit(solution)/shard_map/ppermute | solution.py:28
  369.6 1.7 collective-permute-start.76
  372.9 4.2 collective-permute-done.79
  382.3 2.3 collective-permute-done.83
  386.4 1.9 collective-permute-done.84
  389.7 2.8 collective-permute-start.87
  395.1 2.4 collective-permute-start.80
  397.5 4.4 %collective-permute-start.81 = (bf16[64,1024]{1,0:T(8,128)(2,1)S(1)}, bf16[64,1024]{1,0:T(8,128)(2,1)S(1)}, u32[]{:S(2)}, u32[]{:S(2)}) collective-permute-start(bf16[64,1024]{1,0:T(8,128)(2,1)S(1)} %get-tuple-element.177), channel_id=1, source_target_pairs={{8,0},{4,1},{9,4},{5,5},{24,8},{20,9},{25,12},{21,13},{12,16},{0,1... | collective-permute-start | bytes 393224 | tf_op jit(solution)/shard_map/ppermute | solution.py:106
  404.6 4.3 %collective-permute-done.81 = bf16[64,1024]{1,0:T(8,128)(2,1)S(1)} collective-permute-done((bf16[64,1024]{1,0:T(8,128)(2,1)S(1)}, bf16[64,1024]{1,0:T(8,128)(2,1)S(1)}, u32[]{:S(2)}, u32[]{:S(2)}) %collective-permute-start.81) | collective-permute-done | bytes 131104 | tf_op jit(solution)/shard_map/ppermute | solution.py:106
  416.9 1.8 reshape.492
  419.8 2.3 reshape.490
  (550 shorter events, 150.8 us)
Async XLA Ops:
  7.2 146.4 %all-gather.2.cloned.1.call-start = ((), (), s32[]{:S(2)}) async-start(), calls=%async_computation.3 | async-start | bytes 2228224 | tf_op jit(solution)/shard_map/all_gather | solution.py:427
  8.0 59.6 %collective-permute-start.32 = (bf16[128]{0:T(256)(128)(2,1)S(1)}, bf16[128]{0:T(256)(128)(2,1)S(1)}, u32[]{:S(2)}, u32[]{:S(2)}) collective-permute-start(bf16[128]{0:T(256)(128)(2,1)S(1)} %broadcast_select_fusion.19), channel_id=1, source_target_pairs={{0,12},{4,8},{8,4},{12,0},{1,13},{5,9},{9,5},{13,1},{2,14},{6,10},... | collective-permute-start | bytes 776 | tf_op jit(solution)/shard_map/ppermute | solution.py:28
  13.0 54.6 %collective-permute-start.31 = (bf16[128]{0:T(256)(128)(2,1)S(1)}, bf16[128]{0:T(256)(128)(2,1)S(1)}, u32[]{:S(2)}, u32[]{:S(2)}) collective-permute-start(bf16[128]{0:T(256)(128)(2,1)S(1)} %broadcast_select_fusion.19), channel_id=1, source_target_pairs={{0,8},{4,12},{8,0},{12,4},{1,9},{5,13},{9,1},{13,5},{2,10},{6,14},... | collective-permute-start | bytes 776 | tf_op jit(solution)/shard_map/ppermute | solution.py:28
  13.9 16.3 %collective-permute-start.5 = (bf16[16,64]{1,0:T(8,128)(2,1)S(1)}, bf16[16,64]{1,0:T(8,128)(2,1)S(1)}, u32[]{:S(2)}, u32[]{:S(2)}) collective-permute-start(bf16[16,64]{1,0:T(8,128)(2,1)S(1)} %stack.164), channel_id=1, source_target_pairs={{0,12},{4,8},{8,4},{12,0},{1,13},{5,9},{9,5},{13,1},{2,14},{6,10},... | collective-permute-start | bytes 6152 | tf_op jit(solution)/shard_map/ppermute | solution.py:28
  15.8 15.0 %collective-permute-start.4 = (bf16[16,64]{1,0:T(8,128)(2,1)S(1)}, bf16[16,64]{1,0:T(8,128)(2,1)S(1)}, u32[]{:S(2)}, u32[]{:S(2)}) collective-permute-start(bf16[16,64]{1,0:T(8,128)(2,1)S(1)} %stack.164), channel_id=1, source_target_pairs={{0,8},{4,12},{8,0},{12,4},{1,9},{5,13},{9,1},{13,5},{2,10},{6,14},... | collective-permute-start | bytes 6152 | tf_op jit(solution)/shard_map/ppermute | solution.py:28
  17.6 10.9 %collective-permute-start.2 = (s32[2,2,4]{2,0,1:T(2,128)S(1)}, s32[2,2,4]{2,0,1:T(2,128)S(1)}, u32[]{:S(2)}, u32[]{:S(2)}) collective-permute-start(s32[2,2,4]{2,0,1:T(2,128)S(1)} %pad_add_fusion), channel_id=1, source_target_pairs={{0,16},{16,0},{1,17},{17,1},{2,18},{18,2},{3,19},{19,3},{4,20},{20... | collective-permute-start | bytes 200 | tf_op jit(solution)/shard_map/ppermute | solution.py:28
  23.8 51.0 %all-to-all-start = ((bf16[4,64,896]{2,1,0:T(8,128)(2,1)}), bf16[4,64,896]{2,1,0:T(8,128)(2,1)S(1)}, u32[]{:S(2)}, u32[]{:S(2)}) async-start(bf16[4,64,896]{2,1,0:T(8,128)(2,1)} %pad_maximum_fusion.4), calls=%async_computation | async-start | bytes 917504 | tf_op jit(solution)/shard_map/all_to_all | solution.py:424
  30.1 39.2 %collective-permute-start.30 = (bf16[128]{0:T(256)(128)(2,1)S(1)}, bf16[128]{0:T(256)(128)(2,1)S(1)}, u32[]{:S(2)}, u32[]{:S(2)}) collective-permute-start(bf16[128]{0:T(256)(128)(2,1)S(1)} %broadcast_select_fusion.19), channel_id=1, source_target_pairs={{0,4},{4,0},{8,12},{12,8},{1,5},{5,1},{9,13},{13,9},{2,6},{6,2},{1... | collective-permute-start | bytes 776 | tf_op jit(solution)/shard_map/ppermute | solution.py:28
  30.8 12.3 %collective-permute-start = (bf16[64,1024]{1,0:T(8,128)(2,1)S(1)}, bf16[64,1024]{1,0:T(8,128)(2,1)S(1)}, u32[]{:S(2)}, u32[]{:S(2)}) collective-permute-start(bf16[64,1024]{1,0:T(8,128)(2,1)S(1)} %get-tuple-element.164), channel_id=1, source_target_pairs={{0,4},{1,8},{4,5},{5,9},{8,20},{9,24},{12,21},{13,25},{16,0},{17,1... | collective-permute-start | bytes 393224 | tf_op jit(solution)/shard_map/ppermute | solution.py:93
  43.1 9.4 %collective-permute-start.47 = (bf16[64,1024]{1,0:T(8,128)(2,1)S(1)}, bf16[64,1024]{1,0:T(8,128)(2,1)S(1)}, u32[]{:S(2)}, u32[]{:S(2)}) collective-permute-start(bf16[64,1024]{1,0:T(8,128)(2,1)S(1)} %get-tuple-element.158), channel_id=1, source_target_pairs={{0,8},{1,4},{4,9},{5,5},{8,24},{9,20},{12,25},{13,21},{16,12},{17,... | collective-permute-start | bytes 393224 | tf_op jit(solution)/shard_map/ppermute | solution.py:93
  47.3 10.3 %collective-permute-start.46 = (bf16[64,1024]{1,0:T(8,128)(2,1)S(1)}, bf16[64,1024]{1,0:T(8,128)(2,1)S(1)}, u32[]{:S(2)}, u32[]{:S(2)}) collective-permute-start(bf16[64,1024]{1,0:T(8,128)(2,1)S(1)} %get-tuple-element.159), channel_id=1, source_target_pairs={{0,4},{1,8},{4,5},{5,9},{8,20},{9,24},{12,21},{13,25},{16,0},{17,1... | collective-permute-start | bytes 393224 | tf_op jit(solution)/shard_map/ppermute | solution.py:93
  52.5 19.3 %collective-permute-start.9 = (bf16[128,1024]{1,0:T(8,128)(2,1)S(1)}, bf16[128,1024]{1,0:T(8,128)(2,1)S(1)}, u32[]{:S(2)}, u32[]{:S(2)}) collective-permute-start(bf16[128,1024]{1,0:T(8,128)(2,1)S(1)} %get-tuple-element.206), channel_id=1, source_target_pairs={{0,2},{2,0},{1,3},{3,1},{4,6},{6,4},{5,7},{7,5},{8,10},{10,8},{9,1... | collective-permute-start | bytes 786440 | tf_op jit(solution)/shard_map/ppermute | solution.py:28
  57.6 26.5 %collective-permute-start.8 = (bf16[128,1024]{1,0:T(8,128)(2,1)S(1)}, bf16[128,1024]{1,0:T(8,128)(2,1)}, u32[]{:S(2)}, u32[]{:S(2)}) collective-permute-start(bf16[128,1024]{1,0:T(8,128)(2,1)S(1)} %get-tuple-element.206), channel_id=1, source_target_pairs={{0,1},{1,0},{2,3},{3,2},{4,5},{5,4},{6,7},{7,6},{8,9},{9,8},{10,11... | collective-permute-start | bytes 786440 | tf_op jit(solution)/shard_map/ppermute | solution.py:28
  67.6 9.2 %collective-permute-start.11 = (bf16[128,1024]{1,0:T(8,128)(2,1)S(1)}, bf16[128,1024]{1,0:T(8,128)(2,1)S(1)}, u32[]{:S(2)}, u32[]{:S(2)}) collective-permute-start(bf16[128,1024]{1,0:T(8,128)(2,1)S(1)} %get-tuple-element.206), channel_id=1, source_target_pairs={{0,16},{16,0},{1,17},{17,1},{2,18},{18,2},{3,19},{19,3},{4,20},{20... | collective-permute-start | bytes 786440 | tf_op jit(solution)/shard_map/ppermute | solution.py:28
  67.6 9.2 %collective-permute-start.49 = (bf16[128,1024]{1,0:T(8,128)(2,1)}, bf16[128,1024]{1,0:T(8,128)(2,1)S(1)}, u32[]{:S(2)}, u32[]{:S(2)}) collective-permute-start(bf16[128,1024]{1,0:T(8,128)(2,1)} %pad_maximum_fusion.13), channel_id=1, source_target_pairs={{0,2},{2,0},{1,3},{3,1},{4,6},{6,4},{5,7},{7,5},{8,10},{10,8},{9,1... | collective-permute-start | bytes 786440 | tf_op jit(solution)/shard_map/ppermute | solution.py:28
  69.4 13.0 %collective-permute-start.51 = (bf16[128,1024]{1,0:T(8,128)(2,1)}, bf16[128,1024]{1,0:T(8,128)(2,1)S(1)}, u32[]{:S(2)}, u32[]{:S(2)}) collective-permute-start(bf16[128,1024]{1,0:T(8,128)(2,1)} %pad_maximum_fusion.13), channel_id=1, source_target_pairs={{0,16},{16,0},{1,17},{17,1},{2,18},{18,2},{3,19},{19,3},{4,20},{20... | collective-permute-start | bytes 786440 | tf_op jit(solution)/shard_map/ppermute | solution.py:28
  71.9 14.7 %collective-permute-start.48 = (bf16[128,1024]{1,0:T(8,128)(2,1)}, bf16[128,1024]{1,0:T(8,128)(2,1)}, u32[]{:S(2)}, u32[]{:S(2)}) collective-permute-start(bf16[128,1024]{1,0:T(8,128)(2,1)} %pad_maximum_fusion.13), channel_id=1, source_target_pairs={{0,1},{1,0},{2,3},{3,2},{4,5},{5,4},{6,7},{7,6},{8,9},{9,8},{10,11... | collective-permute-start | bytes 786440 | tf_op jit(solution)/shard_map/ppermute | solution.py:28
  76.8 19.6 %collective-permute-start.28 = (bf16[256,512]{1,0:T(8,128)(2,1)S(1)}, bf16[256,512]{1,0:T(8,128)(2,1)S(1)}, u32[]{:S(2)}, u32[]{:S(2)}) collective-permute-start(bf16[256,512]{1,0:T(8,128)(2,1)S(1)} %slice.552), channel_id=1, source_target_pairs={{0,8},{4,12},{8,0},{12,4},{1,9},{5,13},{9,1},{13,5},{2,10},{6,14},... | collective-permute-start | bytes 786440 | tf_op jit(solution)/shard_map/ppermute | solution.py:28
  76.8 12.7 %collective-permute-start.14 = (bf16[64,1024]{1,0:T(8,128)(2,1)S(1)}, bf16[64,1024]{1,0:T(8,128)(2,1)S(1)}, u32[]{:S(2)}, u32[]{:S(2)}) collective-permute-start(bf16[64,1024]{1,0:T(8,128)(2,1)S(1)} %slice.543), channel_id=1, source_target_pairs={{0,16},{16,0},{1,17},{17,1},{2,18},{18,2},{3,19},{19,3},{4,20},{20... | collective-permute-start | bytes 393224 | tf_op jit(solution)/shard_map/ppermute | solution.py:28
  82.4 9.3 %collective-permute-start.13 = (bf16[64,1024]{1,0:T(8,128)(2,1)S(1)}, bf16[64,1024]{1,0:T(8,128)(2,1)S(1)}, u32[]{:S(2)}, u32[]{:S(2)}) collective-permute-start(bf16[64,1024]{1,0:T(8,128)(2,1)S(1)} %slice.542), channel_id=1, source_target_pairs={{0,2},{2,0},{1,3},{3,1},{4,6},{6,4},{5,7},{7,5},{8,10},{10,8},{9,1... | collective-permute-start | bytes 393224 | tf_op jit(solution)/shard_map/ppermute | solution.py:28
  84.1 9.3 %collective-permute-start.54 = (bf16[64,1024]{1,0:T(8,128)(2,1)S(1)}, bf16[64,1024]{1,0:T(8,128)(2,1)S(1)}, u32[]{:S(2)}, u32[]{:S(2)}) collective-permute-start(bf16[64,1024]{1,0:T(8,128)(2,1)S(1)} %slice.581), channel_id=1, source_target_pairs={{0,16},{16,0},{1,17},{17,1},{2,18},{18,2},{3,19},{19,3},{4,20},{20... | collective-permute-start | bytes 393224 | tf_op jit(solution)/shard_map/ppermute | solution.py:28
  89.5 89.0 %collective-permute-start.35 = (bf16[128,1024]{1,0:T(8,128)(2,1)S(1)}, bf16[128,1024]{1,0:T(8,128)(2,1)}, u32[]{:S(2)}, u32[]{:S(2)}) collective-permute-start(bf16[128,1024]{1,0:T(8,128)(2,1)S(1)} %constant_dynamic-slice_fusion.29), channel_id=1, source_target_pairs={{0,12},{4,8},{8,4},{12,0},{1,13},{5,9},{9,5},{13,1},{2,14},{6,10},... | collective-permute-start | bytes 786440 | tf_op jit(solution)/shard_map/ppermute | solution.py:28
  91.7 42.6 %collective-permute-start.18 = (bf16[256,384]{1,0:T(8,128)(2,1)S(1)}, bf16[256,384]{1,0:T(8,128)(2,1)S(1)}, u32[]{:S(2)}, u32[]{:S(2)}) collective-permute-start(bf16[256,384]{1,0:T(8,128)(2,1)S(1)} %slice.544), channel_id=1, source_target_pairs={{0,12},{4,8},{8,4},{12,0},{1,13},{5,9},{9,5},{13,1},{2,14},{6,10},... | collective-permute-start | bytes 589832 | tf_op jit(solution)/shard_map/ppermute | solution.py:28
  93.4 41.1 %collective-permute-start.17 = (bf16[256,384]{1,0:T(8,128)(2,1)S(1)}, bf16[256,384]{1,0:T(8,128)(2,1)S(1)}, u32[]{:S(2)}, u32[]{:S(2)}) collective-permute-start(bf16[256,384]{1,0:T(8,128)(2,1)S(1)} %slice.544), channel_id=1, source_target_pairs={{0,8},{4,12},{8,0},{12,4},{1,9},{5,13},{9,1},{13,5},{2,10},{6,14},... | collective-permute-start | bytes 589832 | tf_op jit(solution)/shard_map/ppermute | solution.py:28
  93.5 20.9 %collective-permute-start.29 = (bf16[256,512]{1,0:T(8,128)(2,1)S(1)}, bf16[256,512]{1,0:T(8,128)(2,1)S(1)}, u32[]{:S(2)}, u32[]{:S(2)}) collective-permute-start(bf16[256,512]{1,0:T(8,128)(2,1)S(1)} %slice.552), channel_id=1, source_target_pairs={{0,12},{4,8},{8,4},{12,0},{1,13},{5,9},{9,5},{13,1},{2,14},{6,10},... | collective-permute-start | bytes 786440 | tf_op jit(solution)/shard_map/ppermute | solution.py:28
  96.4 19.2 %collective-permute-start.27 = (bf16[256,512]{1,0:T(8,128)(2,1)S(1)}, bf16[256,512]{1,0:T(8,128)(2,1)S(1)}, u32[]{:S(2)}, u32[]{:S(2)}) collective-permute-start(bf16[256,512]{1,0:T(8,128)(2,1)S(1)} %slice.552), channel_id=1, source_target_pairs={{0,4},{4,0},{8,12},{12,8},{1,5},{5,1},{9,13},{13,9},{2,6},{6,2},{1... | collective-permute-start | bytes 786440 | tf_op jit(solution)/shard_map/ppermute | solution.py:28
  116.4 15.8 %collective-permute-start.50 = (bf16[128,1024]{1,0:T(8,128)(2,1)S(1)}, bf16[128,1024]{1,0:T(8,128)(2,1)S(1)}, u32[]{:S(2)}, u32[]{:S(2)}) collective-permute-start(bf16[128,1024]{1,0:T(8,128)(2,1)S(1)} %collective-permute-done.49), channel_id=1, source_target_pairs={{0,1},{1,0},{2,3},{3,2},{4,5},{5,4},{6,7},{7,6},{8,9},{9,8},{10,11... | collective-permute-start | bytes 786440 | tf_op jit(solution)/shard_map/ppermute | solution.py:28
  117.1 20.4 %collective-permute-start.16 = (bf16[256,384]{1,0:T(8,128)(2,1)S(1)}, bf16[256,384]{1,0:T(8,128)(2,1)S(1)}, u32[]{:S(2)}, u32[]{:S(2)}) collective-permute-start(bf16[256,384]{1,0:T(8,128)(2,1)S(1)} %slice.544), channel_id=1, source_target_pairs={{0,4},{4,0},{8,12},{12,8},{1,5},{5,1},{9,13},{13,9},{2,6},{6,2},{1... | collective-permute-start | bytes 589832 | tf_op jit(solution)/shard_map/ppermute | solution.py:28
  133.8 13.6 %collective-permute-start.52 = (bf16[128,1024]{1,0:T(8,128)(2,1)S(1)}, bf16[128,1024]{1,0:T(8,128)(2,1)}, u32[]{:S(2)}, u32[]{:S(2)}) collective-permute-start(bf16[128,1024]{1,0:T(8,128)(2,1)S(1)} %collective-permute-done.51), channel_id=1, source_target_pairs={{0,1},{1,0},{2,3},{3,2},{4,5},{5,4},{6,7},{7,6},{8,9},{9,8},{10,11... | collective-permute-start | bytes 786440 | tf_op jit(solution)/shard_map/ppermute | solution.py:28
  134.3 24.9 %collective-permute-start.55 = (bf16[128,1024]{1,0:T(8,128)(2,1)}, bf16[128,1024]{1,0:T(8,128)(2,1)}, u32[]{:S(2)}, u32[]{:S(2)}) collective-permute-start(bf16[128,1024]{1,0:T(8,128)(2,1)} %pad_maximum_fusion.14), channel_id=1, source_target_pairs={{0,1},{1,0},{2,3},{3,2},{4,5},{5,4},{6,7},{7,6},{8,9},{9,8},{10,11... | collective-permute-start | bytes 786440 | tf_op jit(solution)/shard_map/ppermute | solution.py:28
  143.8 9.6 %all-to-all-start.1 = ((bf16[8,128,128]{2,1,0:T(8,128)(2,1)}), bf16[8,128,128]{2,1,0:T(8,128)(2,1)S(1)}, u32[]{:S(2)}, u32[]{:S(2)}) async-start(bf16[8,128,128]{2,1,0:T(8,128)(2,1)} %get-tuple-element.18), calls=%async_computation.1 | async-start | bytes 524288 | tf_op jit(solution)/shard_map/all_to_all | solution.py:446
  158.7 9.6 %collective-permute-start.19 = (bf16[128,1024]{1,0:T(8,128)(2,1)S(1)}, bf16[128,1024]{1,0:T(8,128)(2,1)S(1)}, u32[]{:S(2)}, u32[]{:S(2)}) collective-permute-start(bf16[128,1024]{1,0:T(8,128)(2,1)S(1)} %get-tuple-element.200), channel_id=1, source_target_pairs={{0,1},{1,0},{2,3},{3,2},{4,5},{5,4},{6,7},{7,6},{8,9},{9,8},{10,11... | collective-permute-start | bytes 786440 | tf_op jit(solution)/shard_map/ppermute | solution.py:28
  158.7 9.1 %collective-permute-start.22 = (bf16[128,1024]{1,0:T(8,128)(2,1)S(1)}, bf16[128,1024]{1,0:T(8,128)(2,1)S(1)}, u32[]{:S(2)}, u32[]{:S(2)}) collective-permute-start(bf16[128,1024]{1,0:T(8,128)(2,1)S(1)} %get-tuple-element.200), channel_id=1, source_target_pairs={{0,16},{16,0},{1,17},{17,1},{2,18},{18,2},{3,19},{19,3},{4,20},{20... | collective-permute-start | bytes 786440 | tf_op jit(solution)/shard_map/ppermute | solution.py:28
  159.2 19.3 %collective-permute-start.34 = (bf16[128,1024]{1,0:T(8,128)(2,1)S(1)}, bf16[128,1024]{1,0:T(8,128)(2,1)S(1)}, u32[]{:S(2)}, u32[]{:S(2)}) collective-permute-start(bf16[128,1024]{1,0:T(8,128)(2,1)S(1)} %constant_dynamic-slice_fusion.29), channel_id=1, source_target_pairs={{0,8},{4,12},{8,0},{12,4},{1,9},{5,13},{9,1},{13,5},{2,10},{6,14},... | collective-permute-start | bytes 786440 | tf_op jit(solution)/shard_map/ppermute | solution.py:28
  170.2 9.7 %collective-permute-start.33 = (bf16[128,1024]{1,0:T(8,128)(2,1)S(1)}, bf16[128,1024]{1,0:T(8,128)(2,1)S(1)}, u32[]{:S(2)}, u32[]{:S(2)}) collective-permute-start(bf16[128,1024]{1,0:T(8,128)(2,1)S(1)} %constant_dynamic-slice_fusion.29), channel_id=1, source_target_pairs={{0,4},{4,0},{8,12},{12,8},{1,5},{5,1},{9,13},{13,9},{2,6},{6,2},{1... | collective-permute-start | bytes 786440 | tf_op jit(solution)/shard_map/ppermute | solution.py:28
  197.9 50.1 %collective-permute-start.92 = (bf16[256,512]{1,0:T(8,128)(2,1)S(1)}, bf16[256,512]{1,0:T(8,128)(2,1)S(1)}, u32[]{:S(2)}, u32[]{:S(2)}) collective-permute-start(bf16[256,512]{1,0:T(8,128)(2,1)S(1)} %pad_maximum_fusion.21), channel_id=1, source_target_pairs={{0,8},{4,12},{8,0},{12,4},{1,9},{5,13},{9,1},{13,5},{2,10},{6,14},... | collective-permute-start | bytes 786440 | tf_op jit(solution)/shard_map/ppermute | solution.py:28
  198.7 50.0 %collective-permute-start.93 = (bf16[256,512]{1,0:T(8,128)(2,1)S(1)}, bf16[256,512]{1,0:T(8,128)(2,1)S(1)}, u32[]{:S(2)}, u32[]{:S(2)}) collective-permute-start(bf16[256,512]{1,0:T(8,128)(2,1)S(1)} %pad_maximum_fusion.22), channel_id=1, source_target_pairs={{0,12},{4,8},{8,4},{12,0},{1,13},{5,9},{9,5},{13,1},{2,14},{6,10},... | collective-permute-start | bytes 786440 | tf_op jit(solution)/shard_map/ppermute | solution.py:28
  204.6 25.1 %collective-permute-start.100 = (bf16[128,1024]{1,0:T(8,128)(2,1)S(1)}, bf16[128,1024]{1,0:T(8,128)(2,1)S(1)}, u32[]{:S(2)}, u32[]{:S(2)}) collective-permute-start(bf16[128,1024]{1,0:T(8,128)(2,1)S(1)} %get-tuple-element.121), channel_id=1, source_target_pairs={{0,4},{4,0},{8,12},{12,8},{1,5},{5,1},{9,13},{13,9},{2,6},{6,2},{1... | collective-permute-start | bytes 786440 | tf_op jit(solution)/shard_map/ppermute | solution.py:28
  205.1 24.6 %collective-permute-start.102 = (bf16[128,1024]{1,0:T(8,128)(2,1)S(1)}, bf16[128,1024]{1,0:T(8,128)(2,1)S(1)}, u32[]{:S(2)}, u32[]{:S(2)}) collective-permute-start(bf16[128,1024]{1,0:T(8,128)(2,1)S(1)} %get-tuple-element.122), channel_id=1, source_target_pairs={{0,12},{4,8},{8,4},{12,0},{1,13},{5,9},{9,5},{13,1},{2,14},{6,10},... | collective-permute-start | bytes 786440 | tf_op jit(solution)/shard_map/ppermute | solution.py:28
  206.7 40.1 %collective-permute-start.101 = (bf16[128,1024]{1,0:T(8,128)(2,1)S(1)}, bf16[128,1024]{1,0:T(8,128)(2,1)S(1)}, u32[]{:S(2)}, u32[]{:S(2)}) collective-permute-start(bf16[128,1024]{1,0:T(8,128)(2,1)S(1)} %get-tuple-element.123), channel_id=1, source_target_pairs={{0,8},{4,12},{8,0},{12,4},{1,9},{5,13},{9,1},{13,5},{2,10},{6,14},... | collective-permute-start | bytes 786440 | tf_op jit(solution)/shard_map/ppermute | solution.py:28
  229.6 20.4 %collective-permute-start.91 = (bf16[256,512]{1,0:T(8,128)(2,1)S(1)}, bf16[256,512]{1,0:T(8,128)(2,1)S(1)}, u32[]{:S(2)}, u32[]{:S(2)}) collective-permute-start(bf16[256,512]{1,0:T(8,128)(2,1)S(1)} %pad_maximum_fusion.20), channel_id=1, source_target_pairs={{0,4},{4,0},{8,12},{12,8},{1,5},{5,1},{9,13},{13,9},{2,6},{6,2},{1... | collective-permute-start | bytes 786440 | tf_op jit(solution)/shard_map/ppermute | solution.py:28
  229.8 44.0 %collective-permute-start.36 = (bf16[128,1024]{1,0:T(8,128)(2,1)S(1)}, bf16[128,1024]{1,0:T(8,128)(2,1)S(1)}, u32[]{:S(2)}, u32[]{:S(2)}) collective-permute-start(bf16[128,1024]{1,0:T(8,128)(2,1)S(1)} %copy-done.19), channel_id=1, source_target_pairs={{0,1},{1,0},{2,3},{3,2},{4,5},{5,4},{6,7},{7,6},{8,9},{9,8},{10,11... | collective-permute-start | bytes 786440 | tf_op jit(solution)/shard_map/ppermute | solution.py:28
  246.8 19.3 %collective-permute-start.56 = (bf16[128,1024]{1,0:T(8,128)(2,1)S(1)}, bf16[128,1024]{1,0:T(8,128)(2,1)S(1)}, u32[]{:S(2)}, u32[]{:S(2)}) collective-permute-start(bf16[128,1024]{1,0:T(8,128)(2,1)S(1)} %get-tuple-element.107), channel_id=1, source_target_pairs={{0,1},{1,0},{2,3},{3,2},{4,5},{5,4},{6,7},{7,6},{8,9},{9,8},{10,11... | collective-permute-start | bytes 786440 | tf_op jit(solution)/shard_map/ppermute | solution.py:28
  250.0 13.5 %collective-permute-start.103 = (bf16[128,1024]{1,0:T(8,128)(2,1)S(1)}, bf16[128,1024]{1,0:T(8,128)(2,1)S(1)}, u32[]{:S(2)}, u32[]{:S(2)}) collective-permute-start(bf16[128,1024]{1,0:T(8,128)(2,1)S(1)} %add_convert_fusion.1), channel_id=1, source_target_pairs={{0,16},{16,0},{1,17},{17,1},{2,18},{18,2},{3,19},{19,3},{4,20},{20... | collective-permute-start | bytes 786440 | tf_op jit(solution)/shard_map/ppermute | solution.py:28
  254.3 8.4 %collective-permute-start.59 = (bf16[64,1024]{1,0:T(8,128)(2,1)S(1)}, bf16[64,1024]{1,0:T(8,128)(2,1)S(1)}, u32[]{:S(2)}, u32[]{:S(2)}) collective-permute-start(bf16[64,1024]{1,0:T(8,128)(2,1)S(1)} %get-tuple-element.180), channel_id=1, source_target_pairs={{0,16},{16,0},{1,17},{17,1},{2,18},{18,2},{3,19},{19,3},{4,20},{20... | collective-permute-start | bytes 393224 | tf_op jit(solution)/shard_map/ppermute | solution.py:28
  260.0 13.7 %collective-permute-start.43 = (bf16[128,1024]{1,0:T(8,128)(2,1)S(1)}, bf16[128,1024]{1,0:T(8,128)(2,1)S(1)}, u32[]{:S(2)}, u32[]{:S(2)}) collective-permute-start(bf16[128,1024]{1,0:T(8,128)(2,1)S(1)} %pad_maximum_fusion.11), channel_id=1, source_target_pairs={{0,16},{16,0},{1,17},{17,1},{2,18},{18,2},{3,19},{19,3},{4,20},{20... | collective-permute-start | bytes 786440 | tf_op jit(solution)/shard_map/ppermute | solution.py:28
  262.8 10.8 %collective-permute-start.63 = (bf16[128,1024]{1,0:T(8,128)(2,1)S(1)}, bf16[128,1024]{1,0:T(8,128)(2,1)S(1)}, u32[]{:S(2)}, u32[]{:S(2)}) collective-permute-start(bf16[128,1024]{1,0:T(8,128)(2,1)S(1)} %pad_maximum_fusion.16), channel_id=1, source_target_pairs={{0,16},{16,0},{1,17},{17,1},{2,18},{18,2},{3,19},{19,3},{4,20},{20... | collective-permute-start | bytes 786440 | tf_op jit(solution)/shard_map/ppermute | solution.py:28
  263.5 10.0 %collective-permute-start.60 = (bf16[128,1024]{1,0:T(8,128)(2,1)S(1)}, bf16[128,1024]{1,0:T(8,128)(2,1)S(1)}, u32[]{:S(2)}, u32[]{:S(2)}) collective-permute-start(bf16[128,1024]{1,0:T(8,128)(2,1)S(1)} %pad_maximum_fusion.15), channel_id=1, source_target_pairs={{0,2},{2,0},{1,3},{3,1},{4,6},{6,4},{5,7},{7,5},{8,10},{10,8},{9,1... | collective-permute-start | bytes 786440 | tf_op jit(solution)/shard_map/ppermute | solution.py:28
  266.1 10.2 %collective-permute-start.40 = (bf16[128,1024]{1,0:T(8,128)(2,1)S(1)}, bf16[128,1024]{1,0:T(8,128)(2,1)S(1)}, u32[]{:S(2)}, u32[]{:S(2)}) collective-permute-start(bf16[128,1024]{1,0:T(8,128)(2,1)S(1)} %pad_maximum_fusion.10), channel_id=1, source_target_pairs={{0,2},{2,0},{1,3},{3,1},{4,6},{6,4},{5,7},{7,5},{8,10},{10,8},{9,1... | collective-permute-start | bytes 786440 | tf_op jit(solution)/shard_map/ppermute | solution.py:28
  280.4 8.8 %collective-permute-start.64 = (bf16[128,1024]{1,0:T(8,128)(2,1)}, bf16[128,1024]{1,0:T(8,128)(2,1)}, u32[]{:S(2)}, u32[]{:S(2)}) collective-permute-start(bf16[128,1024]{1,0:T(8,128)(2,1)} %get-tuple-element.92), channel_id=1, source_target_pairs={{0,1},{1,0},{2,3},{3,2},{4,5},{5,4},{6,7},{7,6},{8,9},{9,8},{10,11... | collective-permute-start | bytes 786440 | tf_op jit(solution)/shard_map/ppermute | solution.py:28
  316.7 15.2 %collective-permute-start.77 = (bf16[128,1024]{1,0:T(8,128)(2,1)}, bf16[128,1024]{1,0:T(8,128)(2,1)S(1)}, u32[]{:S(2)}, u32[]{:S(2)}) collective-permute-start(bf16[128,1024]{1,0:T(8,128)(2,1)} %get-tuple-element.101), channel_id=1, source_target_pairs={{0,1},{1,0},{2,3},{3,2},{4,5},{5,4},{6,7},{7,6},{8,9},{9,8},{10,11... | collective-permute-start | bytes 786440 | tf_op jit(solution)/shard_map/ppermute | solution.py:28
  316.8 15.3 %collective-permute-start.74 = (bf16[128,1024]{1,0:T(8,128)(2,1)S(1)}, bf16[128,1024]{1,0:T(8,128)(2,1)S(1)}, u32[]{:S(2)}, u32[]{:S(2)}) collective-permute-start(bf16[128,1024]{1,0:T(8,128)(2,1)S(1)} %get-tuple-element.102), channel_id=1, source_target_pairs={{0,1},{1,0},{2,3},{3,2},{4,5},{5,4},{6,7},{7,6},{8,9},{9,8},{10,11... | collective-permute-start | bytes 786440 | tf_op jit(solution)/shard_map/ppermute | solution.py:28
  317.3 17.4 %collective-permute-start.73 = (bf16[128,1024]{1,0:T(8,128)(2,1)S(1)}, bf16[128,1024]{1,0:T(8,128)(2,1)S(1)}, u32[]{:S(2)}, u32[]{:S(2)}) collective-permute-start(bf16[128,1024]{1,0:T(8,128)(2,1)S(1)} %get-tuple-element.103), channel_id=1, source_target_pairs={{0,1},{1,0},{2,3},{3,2},{4,5},{5,4},{6,7},{7,6},{8,9},{9,8},{10,11... | collective-permute-start | bytes 786440 | tf_op jit(solution)/shard_map/ppermute | solution.py:28
  325.5 77.6 %collective-permute-start.44 = (bf16[64,1024]{1,0:T(8,128)(2,1)}, bf16[64,1024]{1,0:T(8,128)(2,1)}, u32[]{:S(2)}, u32[]{:S(2)}) collective-permute-start(bf16[64,1024]{1,0:T(8,128)(2,1)} %get-tuple-element.186), channel_id=1, source_target_pairs={{4,0},{8,1},{5,4},{9,5},{20,8},{24,9},{21,12},{25,13},{0,16},{12,1... | collective-permute-start | bytes 393224 | tf_op jit(solution)/shard_map/ppermute | solution.py:106
  328.3 74.8 %collective-permute-start.45 = (bf16[64,1024]{1,0:T(8,128)(2,1)S(1)}, bf16[64,1024]{1,0:T(8,128)(2,1)}, u32[]{:S(2)}, u32[]{:S(2)}) collective-permute-start(bf16[64,1024]{1,0:T(8,128)(2,1)S(1)} %get-tuple-element.187), channel_id=1, source_target_pairs={{8,0},{4,1},{9,4},{5,5},{24,8},{20,9},{25,12},{21,13},{12,16},{0,1... | collective-permute-start | bytes 393224 | tf_op jit(solution)/shard_map/ppermute | solution.py:106
  332.0 15.3 %collective-permute-start.88 = (bf16[256,384]{1,0:T(8,128)(2,1)}, bf16[256,384]{1,0:T(8,128)(2,1)S(1)}, u32[]{:S(2)}, u32[]{:S(2)}) collective-permute-start(bf16[256,384]{1,0:T(8,128)(2,1)} %get-tuple-element.138), channel_id=1, source_target_pairs={{0,4},{4,0},{8,12},{12,8},{1,5},{5,1},{9,13},{13,9},{2,6},{6,2},{1... | collective-permute-start | bytes 589832 | tf_op jit(solution)/shard_map/ppermute | solution.py:28
  332.1 15.2 %collective-permute-start.90 = (bf16[256,384]{1,0:T(8,128)(2,1)}, bf16[256,384]{1,0:T(8,128)(2,1)S(1)}, u32[]{:S(2)}, u32[]{:S(2)}) collective-permute-start(bf16[256,384]{1,0:T(8,128)(2,1)} %get-tuple-element.139), channel_id=1, source_target_pairs={{0,12},{4,8},{8,4},{12,0},{1,13},{5,9},{9,5},{13,1},{2,14},{6,10},... | collective-permute-start | bytes 589832 | tf_op jit(solution)/shard_map/ppermute | solution.py:28
  335.4 21.4 %collective-permute-start.89 = (bf16[256,384]{1,0:T(8,128)(2,1)}, bf16[256,384]{1,0:T(8,128)(2,1)S(1)}, u32[]{:S(2)}, u32[]{:S(2)}) collective-permute-start(bf16[256,384]{1,0:T(8,128)(2,1)} %get-tuple-element.140), channel_id=1, source_target_pairs={{0,8},{4,12},{8,0},{12,4},{1,9},{5,13},{9,1},{13,5},{2,10},{6,14},... | collective-permute-start | bytes 589832 | tf_op jit(solution)/shard_map/ppermute | solution.py:28
  347.3 25.7 %collective-permute-start.72 = (bf16[128,1024]{1,0:T(8,128)(2,1)}, bf16[128,1024]{1,0:T(8,128)(2,1)}, u32[]{:S(2)}, u32[]{:S(2)}) collective-permute-start(bf16[128,1024]{1,0:T(8,128)(2,1)} %get-tuple-element.100), channel_id=1, source_target_pairs={{0,1},{1,0},{2,3},{3,2},{4,5},{5,4},{6,7},{7,6},{8,9},{9,8},{10,11... | collective-permute-start | bytes 786440 | tf_op jit(solution)/shard_map/ppermute | solution.py:28
  347.3 22.3 %collective-permute-start.99 = (bf16[64,512]{1,0:T(8,128)(2,1)S(1)}, bf16[64,512]{1,0:T(8,128)(2,1)}, u32[]{:S(2)}, u32[]{:S(2)}) collective-permute-start(bf16[64,512]{1,0:T(8,128)(2,1)S(1)} %fusion.51), channel_id=1, source_target_pairs={{0,16},{16,0},{1,17},{17,1},{2,18},{18,2},{3,19},{19,3},{4,20},{20... | collective-permute-start | bytes 196616 | tf_op jit(solution)/shard_map/ppermute | solution.py:28
  359.7 33.2 %all-to-all-start.2 = ((bf16[4,64,896]{2,1,0:T(8,128)(2,1)}), bf16[4,64,896]{2,1,0:T(8,128)(2,1)S(1)}, u32[]{:S(2)}, u32[]{:S(2)}) async-start(bf16[4,64,896]{2,1,0:T(8,128)(2,1)} %pad_maximum_fusion.5), calls=%async_computation.2 | async-start | bytes 917504 | tf_op jit(solution)/shard_map/all_to_all | solution.py:495
  393.0 19.2 %collective-permute-start.94 = (bf16[4,64,896]{2,1,0:T(8,128)(2,1)S(1)}, bf16[4,64,896]{2,1,0:T(8,128)(2,1)S(1)}, u32[]{:S(2)}, u32[]{:S(2)}) collective-permute-start(bf16[4,64,896]{2,1,0:T(8,128)(2,1)S(1)} %all-to-all-done.2), channel_id=1, source_target_pairs={{0,16},{16,0},{1,17},{17,1},{2,18},{18,2},{3,19},{19,3},{4,20},{20... | collective-permute-start | bytes 1376264 | tf_op jit(solution)/shard_map/ppermute | solution.py:28
  395.1 9.5 %collective-permute-start.80 = (bf16[64,1024]{1,0:T(8,128)(2,1)S(1)}, bf16[64,1024]{1,0:T(8,128)(2,1)S(1)}, u32[]{:S(2)}, u32[]{:S(2)}) collective-permute-start(bf16[64,1024]{1,0:T(8,128)(2,1)S(1)} %get-tuple-element.176), channel_id=1, source_target_pairs={{4,0},{8,1},{5,4},{9,5},{20,8},{24,9},{21,12},{25,13},{0,16},{12,1... | collective-permute-start | bytes 393224 | tf_op jit(solution)/shard_map/ppermute | solution.py:106
  397.5 11.5 %collective-permute-start.81 = (bf16[64,1024]{1,0:T(8,128)(2,1)S(1)}, bf16[64,1024]{1,0:T(8,128)(2,1)S(1)}, u32[]{:S(2)}, u32[]{:S(2)}) collective-permute-start(bf16[64,1024]{1,0:T(8,128)(2,1)S(1)} %get-tuple-element.177), channel_id=1, source_target_pairs={{8,0},{4,1},{9,4},{5,5},{24,8},{20,9},{25,12},{21,13},{12,16},{0,1... | collective-permute-start | bytes 393224 | tf_op jit(solution)/shard_map/ppermute | solution.py:106
  (110 other events, 747.9 us)
Sparse Core Ops, SparseCore 0:
  17.0 46.4 all-gather.1
